TPU v7x, 256 devices: a whole 4x4x8 slice. The times are simulated.
256 devices in a mesh: ens: 2 (over x_hi), lat: 4 (over x_lo, core), lon: 32 (over y, z).
Axes of the slice: x: 4 (x_hi: 2, x_lo: 2; x = x_hi * 2 + x_lo), y: 4, z: 8, core: 2. Of those that a mesh axis runs over, the one named last changes fastest.
Arguments:
- members_in: bfloat16 [8, 32, 512, 256], P('ens', 'lat', 'lon'), may hold values from -6 to 6
- out_grad: bfloat16 [8, 32, 512, 256], P('ens', 'lat', 'lon'), may hold values from -6 to 6
- weight: bfloat16 [9, 256, 256], replicated, may hold values from -0.125 to 0.125
- basis_blocks: float32 [8, 9, 3, 9], replicated, may hold values from -1.75 to 1.75
- cycle_block: int32 [32], replicated, may hold values from 0 to 7
- half_width: int32 [32, 3], replicated, may hold values from 1 to 4
Outputs:
- result: bfloat16 [8, 32, 512, 256], P('ens', 'lat', 'lon')
- in_grad: bfloat16 [8, 32, 512, 256], P('ens', 'lat', 'lon')
- weight_grad: float32 [9, 256, 256], P(None, 'lon')
All inputs are finite; a program needn't handle non-finite values.
Results may differ from a plain program's by a relative error of at most 0.015.
Values may be sent and summed in bfloat16 or wider, within the bound.
No kernel may reach another device: no remote copies, remote signals or barrier semaphores. Data moves between devices by JAX's collectives and lax.ppermute only.
A program may use at most 64 MiB of HBM per device.

v0:
```python
import math

import jax
import jax.numpy as jnp
from jax import lax
from jax.sharding import PartitionSpec as P

C = 256
K = 9
R = 1
H = 4


def extended(block, sides, width, periodic):
    for axis, dim in sides:
        count = lax.axis_size(axis)
        forward = [(i, i + 1) for i in range(count - 1)]
        if periodic:
            forward.append((count - 1, 0))
        backward = [(target, source) for source, target in forward]
        low = lax.ppermute(
            lax.slice_in_dim(block, block.shape[dim] - width, None, axis=dim), axis, forward
        )
        high = lax.ppermute(lax.slice_in_dim(block, 0, width, axis=dim), axis, backward)
        block = jnp.concatenate([low, block, high], axis=dim)
    return block


def local_table(basis_blocks, cycle_block, half_width, first_cycle, cycle_count):
    total_cycles = cycle_block.shape[0]
    cycle_ids = jnp.clip(
        first_cycle + jnp.arange(cycle_count, dtype=jnp.int32), 0, total_cycles - 1
    )
    one_hot = (cycle_ids[:, None] == jnp.arange(total_cycles, dtype=jnp.int32)[None, :]).astype(
        jnp.int32
    )
    block_ids = jnp.sum(one_hot * cycle_block[None, :], axis=1)
    widths = jnp.sum(one_hot[:, :, None] * half_width[None, :, :], axis=1)
    block_count = basis_blocks.shape[0]
    pick_block = (block_ids[:, None] == jnp.arange(block_count, dtype=jnp.int32)[None, :]).astype(
        jnp.float32
    )
    picked = jnp.dot(
        pick_block,
        basis_blocks.reshape(block_count, -1),
        precision=lax.Precision.HIGHEST,
        preferred_element_type=jnp.float32,
    )
    picked = picked.reshape((cycle_count,) + basis_blocks.shape[1:])
    offsets = jnp.arange(2 * H + 1, dtype=jnp.int32) - H
    inside = jnp.abs(offsets)[None, None, :] <= widths[:, :, None]
    return (jnp.where(inside[:, None, :, :], picked, jnp.float32(0.0)), widths)


def extend(values):
    tall_block = extended(values, (("lat", 1),), R, False)
    return extended(tall_block, (("lon", 2),), H, True)


def spread_forward(padded, coefficients, half_reach):
    lat_rows = padded.shape[1] - 2 * R
    lon_cols = padded.shape[2] - 2 * H

    def single(member):
        summed = jnp.zeros(
            (lat_rows, lon_cols, coefficients.shape[1], member.shape[-1]), jnp.float32
        )
        for offset_row in range(2 * R + 1):
            for offset_col in range(H - half_reach, H + half_reach + 1):
                sliced = member[
                    offset_row : offset_row + lat_rows, offset_col : offset_col + lon_cols
                ]
                summed = summed + coefficients[:, None, :, offset_row, offset_col, None] * sliced[
                    :, :, None, :
                ].astype(jnp.float32)
        return summed.astype(jnp.bfloat16)

    return lax.map(single, padded)


def spread_adjoint(padded, coefficients, half_reach):
    lat_rows = padded.shape[1] - 2 * R
    lon_cols = padded.shape[2] - 2 * H

    def single(member):
        summed = jnp.zeros(
            (lat_rows, lon_cols, coefficients.shape[1], member.shape[-1]), jnp.float32
        )
        for offset_row in range(2 * R + 1):
            lead_row = 2 * R - offset_row
            rows_coef = coefficients[lead_row : lead_row + lat_rows]
            for offset_col in range(H - half_reach, H + half_reach + 1):
                lead_col = 2 * H - offset_col
                sliced = member[lead_row : lead_row + lat_rows, lead_col : lead_col + lon_cols]
                summed = summed + rows_coef[:, None, :, offset_row, offset_col, None] * sliced[
                    :, :, None, :
                ].astype(jnp.float32)
        return summed.astype(jnp.bfloat16)

    return lax.map(single, padded)


def apply_spread(kernel, padded, coefficients):
    return kernel(padded, coefficients, H)


def shards(members_in, out_grad, weight, basis_blocks, cycle_block, half_width):
    members, lat_rows, lon_cols, channels = members_in.shape
    first_cycle = lax.axis_index("lat") * lat_rows
    wide_coef, wide_widths = local_table(
        basis_blocks, cycle_block, half_width, first_cycle - R, lat_rows + 2 * R
    )
    own_coef = wide_coef[R : R + lat_rows]
    padded_in = extend(members_in)
    features = apply_spread(spread_forward, padded_in, own_coef)
    feature_rows = features.reshape(members * lat_rows * lon_cols, K * C)
    mixed = jnp.dot(feature_rows, weight.reshape(K * C, C), preferred_element_type=jnp.float32)
    activated, slope_fn = jax.vjp(jax.nn.gelu, mixed)
    cot_rows = out_grad.reshape(-1, channels).astype(jnp.float32)
    result = (members_in.reshape(-1, channels).astype(jnp.float32) + activated).astype(jnp.bfloat16)
    grad_mixed = slope_fn(cot_rows)[0].astype(jnp.bfloat16)
    cell_count = (
        members
        * lax.axis_size("ens")
        * lat_rows
        * lax.axis_size("lat")
        * lon_cols
        * lax.axis_size("lon")
    )
    local_grad = lax.dot_general(
        feature_rows, grad_mixed, (((0,), (0,)), ((), ())), preferred_element_type=jnp.float32
    )
    local_grad = (local_grad * (1.0 / math.sqrt(cell_count))).reshape(K, C, C)
    share_size = channels // lax.axis_size("lon")
    summed_grad = lax.psum(local_grad, ("ens", "lat", "lon"))
    weight_grad = lax.dynamic_slice_in_dim(
        summed_grad, lax.axis_index("lon") * share_size, share_size, 1
    )
    padded_grad = extend(grad_mixed.reshape(members, lat_rows, lon_cols, channels))
    back = apply_spread(spread_adjoint, padded_grad, wide_coef)
    branch_rows = lax.dot_general(
        back.reshape(-1, K, C),
        weight,
        (((1, 2), (0, 2)), ((), ())),
        preferred_element_type=jnp.float32,
    )
    in_grad = (cot_rows + branch_rows).astype(jnp.bfloat16)
    return (result.reshape(members_in.shape), in_grad.reshape(members_in.shape), weight_grad)


def solution(mesh):
    return jax.shard_map(
        shards,
        mesh=mesh,
        in_specs=(P("ens", "lat", "lon", None), P("ens", "lat", "lon", None), P(), P(), P(), P()),
        out_specs=(
            P("ens", "lat", "lon", None),
            P("ens", "lat", "lon", None),
            P(None, "lon", None),
        ),
        check_vma=False,
    )
```

profile of v0, /device:TPU:1, one launch (start us, length us, event | category | flops | bytes accessed | tf_op | source)
XLA Modules:
  0.0 345.7 jit_solution(58817412065547863)
XLA Ops:
  8.1 5.1 %collective-permute-start.1 = (bf16[4,1,16,256]{3,2,1,0:T(8,128)(2,1)S(1)}, bf16[4,1,16,256]{3,2,1,0:T(8,128)(2,1)S(1)}, u32[]{:S(2)}, u32[]{:S(2)}) collective-permute-start(bf16[4,1,16,256]{3,2,1,0:T(8,128)(2,1)S(1)} %get-tuple-element.205), channel_id=1, source_target_pairs={{32,0},{64,32},{96,64},{33,1},{65,33},{97,65},{34,2},{66,34},{98,6... | collective-permute-start | bytes 98312 | tf_op jit(solution)/shard_map/ppermute | solution.py:24
  13.2 1.9 collective-permute-start
  20.6 6.5 %collective-permute-start.3 = (bf16[4,10,4,256]{3,2,1,0:T(4,128)(2,1)S(1)}, bf16[4,10,4,256]{3,2,1,0:T(4,128)(2,1)S(1)}, u32[]{:S(2)}, u32[]{:S(2)}) collective-permute-start(bf16[4,10,4,256]{3,2,1,0:T(4,128)(2,1)S(1)} %get-tuple-element.202), channel_id=1, source_target_pairs={{1,0},{2,1},{3,2},{4,3},{5,4},{6,5},{7,6},{8,7},{9,8},{10,9},{11,1... | collective-permute-start | bytes 245768 | tf_op jit(solution)/shard_map/ppermute | solution.py:24
  29.5 2.4 broadcast.874.clone
  32.0 25.8 %while.20 = (s32[]{:T(128)}, bf16[4,8,16,9,256]{4,3,2,1,0:T(8,128)(2,1)}, f32[8,9,3,9]{1,0,3,2:T(8,128)S(1)}, bf16[4,10,24,256]{3,2,1,0:T(8,128)(2,1)S(1)}, s32[]{:T(128)}) while((s32[]{:T(128)}, bf16[4,8,16,9,256]{4,3,2,1,0:T(8,128)(2,1)}, f32[8,9,3,9]{1,0,3,2:T(8,128)S(1)}, bf16[4,10,24,256]{3,2,1,0:T(8,128)(2,1)S(1)}, s32[]{:T(128)}) %tuple.162), condition=%wide.region_3.4_spmd, body=%wide.region_2.3_spmd.sunk | while | flops 16809984 | bytes 10165101 | solution.py:78
  32.5 6.0 %fusion.39 = bf16[4,8,16,9,256]{4,3,2,1,0:T(8,128)(2,1)} fusion(bf16[4,8,16,9,256]{4,3,2,1,0:T(8,128)(2,1)} %get-tuple-element.479, s32[]{:T(128)S(6)} %copy.43, f32[8,16,256]{2,1,0:T(8,128)S(1)} %get-tuple-element.361, f32[8,9]{1,0:T(8,128)S(1)} %get-tuple-element.362, f32[8,16,256]{2,1,0:T(8,128)S(1)} %get-tuple-element.363, ...), kind=kLoop, calls=%fused_computation.1.clone.1 | loop fusion | flops 15925248 | bytes 4595300 | tf_op jit(solution)/shard_map/while/body/jit(dynamic_update_index_in_dim)/dynamic_update_slice | solution.py:78
  38.9 6.0 %fusion.39 = bf16[4,8,16,9,256]{4,3,2,1,0:T(8,128)(2,1)} fusion(bf16[4,8,16,9,256]{4,3,2,1,0:T(8,128)(2,1)} %get-tuple-element.479, s32[]{:T(128)S(6)} %copy.43, f32[8,16,256]{2,1,0:T(8,128)S(1)} %get-tuple-element.361, f32[8,9]{1,0:T(8,128)S(1)} %get-tuple-element.362, f32[8,16,256]{2,1,0:T(8,128)S(1)} %get-tuple-element.363, ...), kind=kLoop, calls=%fused_computation.1.clone.1 | loop fusion | flops 15925248 | bytes 4595300 | tf_op jit(solution)/shard_map/while/body/jit(dynamic_update_index_in_dim)/dynamic_update_slice | solution.py:78
  45.3 6.0 %fusion.39 = bf16[4,8,16,9,256]{4,3,2,1,0:T(8,128)(2,1)} fusion(bf16[4,8,16,9,256]{4,3,2,1,0:T(8,128)(2,1)} %get-tuple-element.479, s32[]{:T(128)S(6)} %copy.43, f32[8,16,256]{2,1,0:T(8,128)S(1)} %get-tuple-element.361, f32[8,9]{1,0:T(8,128)S(1)} %get-tuple-element.362, f32[8,16,256]{2,1,0:T(8,128)S(1)} %get-tuple-element.363, ...), kind=kLoop, calls=%fused_computation.1.clone.1 | loop fusion | flops 15925248 | bytes 4595300 | tf_op jit(solution)/shard_map/while/body/jit(dynamic_update_index_in_dim)/dynamic_update_slice | solution.py:78
  51.8 6.0 %fusion.39 = bf16[4,8,16,9,256]{4,3,2,1,0:T(8,128)(2,1)} fusion(bf16[4,8,16,9,256]{4,3,2,1,0:T(8,128)(2,1)} %get-tuple-element.479, s32[]{:T(128)S(6)} %copy.43, f32[8,16,256]{2,1,0:T(8,128)S(1)} %get-tuple-element.361, f32[8,9]{1,0:T(8,128)S(1)} %get-tuple-element.362, f32[8,16,256]{2,1,0:T(8,128)S(1)} %get-tuple-element.363, ...), kind=kLoop, calls=%fused_computation.1.clone.1 | loop fusion | flops 15925248 | bytes 4595300 | tf_op jit(solution)/shard_map/while/body/jit(dynamic_update_index_in_dim)/dynamic_update_slice | solution.py:78
  57.7 3.5 %copy.26 = bf16[64,8,9,256]{3,1,2,0:T(8,128)(2,1)S(1)} copy(bf16[64,8,9,256]{3,2,1,0:T(8,128)(2,1)} %bitcast.159) | data formatting | bytes 4718592
  61.3 1.8 fusion.19
  63.1 2.8 collective-permute-start.4
  65.9 1.9 collective-permute-start.5
  68.3 2.9 collective-permute-done.5
  71.3 5.4 %collective-permute-start.7 = (bf16[4,10,4,256]{3,2,1,0:T(4,128)(2,1)S(1)}, bf16[4,10,4,256]{3,2,1,0:T(4,128)(2,1)S(1)}, u32[]{:S(2)}, u32[]{:S(2)}) collective-permute-start(bf16[4,10,4,256]{3,2,1,0:T(4,128)(2,1)S(1)} %get-tuple-element.200), channel_id=1, source_target_pairs={{1,0},{2,1},{3,2},{4,3},{5,4},{6,5},{7,6},{8,7},{9,8},{10,9},{11,1... | collective-permute-start | bytes 245768 | tf_op jit(solution)/shard_map/ppermute | solution.py:24
  76.7 3.9 %convolution_multiply_fusion = f32[2304,256]{1,0:T(8,128)} fusion(bf16[512,2304]{1,0:T(8,128)(2,1)} %bitcast.162, bf16[512,256]{1,0:T(8,128)(2,1)S(1)} %get-tuple-element.197), kind=kOutput, calls=%fused_computation.114 | convolution fusion | flops 604569600 | bytes 4980736 | tf_op jit(solution)/shard_map/dot_general | solution.py:130
  81.0 2.4 broadcast.874
  83.4 25.5 %while.21 = (s32[]{:T(128)}, bf16[4,8,16,9,256]{4,3,2,1,0:T(8,128)(2,1)}, f32[10,9,3,9]{1,0,3,2:T(8,128)S(1)}, bf16[4,10,24,256]{3,2,1,0:T(8,128)(2,1)S(1)}, s32[]{:T(128)}) while((s32[]{:T(128)}, bf16[4,8,16,9,256]{4,3,2,1,0:T(8,128)(2,1)}, f32[10,9,3,9]{1,0,3,2:T(8,128)S(1)}, bf16[4,10,24,256]{3,2,1,0:T(8,128)(2,1)S(1)}, s32[]{:T(128)}) %tuple.165), condition=%wide.region_5.6_spmd, body=%wide.region_4.5_spmd.sunk | while | flops 16809984 | bytes 10165101 | solution.py:100
  83.9 5.9 %fusion.40 = bf16[4,8,16,9,256]{4,3,2,1,0:T(8,128)(2,1)} fusion(bf16[4,8,16,9,256]{4,3,2,1,0:T(8,128)(2,1)} %get-tuple-element.494, s32[]{:T(128)S(6)} %copy.49, f32[8,16,256]{2,1,0:T(8,128)S(1)} %get-tuple-element.419, f32[8,9]{1,0:T(8,128)S(1)} %get-tuple-element.420, f32[8,16,256]{2,1,0:T(8,128)S(1)} %get-tuple-element.421, ...), kind=kLoop, calls=%fused_computation.58.clone.1 | loop fusion | flops 15925248 | bytes 4595300 | tf_op jit(solution)/shard_map/while/body/jit(dynamic_update_index_in_dim)/dynamic_update_slice | solution.py:78
  90.3 5.9 %fusion.40 = bf16[4,8,16,9,256]{4,3,2,1,0:T(8,128)(2,1)} fusion(bf16[4,8,16,9,256]{4,3,2,1,0:T(8,128)(2,1)} %get-tuple-element.494, s32[]{:T(128)S(6)} %copy.49, f32[8,16,256]{2,1,0:T(8,128)S(1)} %get-tuple-element.419, f32[8,9]{1,0:T(8,128)S(1)} %get-tuple-element.420, f32[8,16,256]{2,1,0:T(8,128)S(1)} %get-tuple-element.421, ...), kind=kLoop, calls=%fused_computation.58.clone.1 | loop fusion | flops 15925248 | bytes 4595300 | tf_op jit(solution)/shard_map/while/body/jit(dynamic_update_index_in_dim)/dynamic_update_slice | solution.py:78
  96.7 5.9 %fusion.40 = bf16[4,8,16,9,256]{4,3,2,1,0:T(8,128)(2,1)} fusion(bf16[4,8,16,9,256]{4,3,2,1,0:T(8,128)(2,1)} %get-tuple-element.494, s32[]{:T(128)S(6)} %copy.49, f32[8,16,256]{2,1,0:T(8,128)S(1)} %get-tuple-element.419, f32[8,9]{1,0:T(8,128)S(1)} %get-tuple-element.420, f32[8,16,256]{2,1,0:T(8,128)S(1)} %get-tuple-element.421, ...), kind=kLoop, calls=%fused_computation.58.clone.1 | loop fusion | flops 15925248 | bytes 4595300 | tf_op jit(solution)/shard_map/while/body/jit(dynamic_update_index_in_dim)/dynamic_update_slice | solution.py:78
  103.0 5.9 %fusion.40 = bf16[4,8,16,9,256]{4,3,2,1,0:T(8,128)(2,1)} fusion(bf16[4,8,16,9,256]{4,3,2,1,0:T(8,128)(2,1)} %get-tuple-element.494, s32[]{:T(128)S(6)} %copy.49, f32[8,16,256]{2,1,0:T(8,128)S(1)} %get-tuple-element.419, f32[8,9]{1,0:T(8,128)S(1)} %get-tuple-element.420, f32[8,16,256]{2,1,0:T(8,128)S(1)} %get-tuple-element.421, ...), kind=kLoop, calls=%fused_computation.58.clone.1 | loop fusion | flops 15925248 | bytes 4595300 | tf_op jit(solution)/shard_map/while/body/jit(dynamic_update_index_in_dim)/dynamic_update_slice | solution.py:78
  108.9 4.4 %fusion.10 = bf16[512,256]{1,0:T(8,128)(2,1)} fusion(bf16[9,256,256]{2,1,0:T(8,128)(2,1)S(1)} %copy-done, bf16[512,9,256]{2,1,0:T(8,128)(2,1)} %bitcast.160, bf16[512,256]{1,0:T(8,128)(2,1)S(1)} %bitcast.168), kind=kOutput, calls=%fused_computation.119 | convolution fusion | flops 604372992 | bytes 4063232 | tf_op jit(solution)/shard_map/dot_general | solution.py:141
  113.3 224.0 %all-reduce.2.cloned.1.call-done = f32[9,256,256]{2,1,0:T(8,128)} async-done(((f32[9,256,256]{2,1,0:T(8,128)}), f32[9,256,256]{2,1,0:T(8,128)}) %all-reduce.2.cloned.1.call-update) | async-done | bytes 2359312 | tf_op jit(solution)/shard_map/psum | solution.py:135
  (83 shorter events, 14.8 us)
Async XLA Ops:
  7.2 54.1 %copy-start = (bf16[9,256,256]{2,1,0:T(8,128)(2,1)S(1)}, bf16[9,256,256]{2,1,0:T(8,128)(2,1)}, u32[]{:S(2)}) copy-start(bf16[9,256,256]{2,1,0:T(8,128)(2,1)} %param.12) | copy-start | bytes 3538948
  7.2 330.2 %all-reduce.2.cloned.1.call-start = ((), (), s32[]{:S(2)}) async-start(), calls=%async_computation | async-start | bytes 4718592 | tf_op jit(solution)/shard_map/psum | solution.py:135
  8.1 11.3 %collective-permute-start.1 = (bf16[4,1,16,256]{3,2,1,0:T(8,128)(2,1)S(1)}, bf16[4,1,16,256]{3,2,1,0:T(8,128)(2,1)S(1)}, u32[]{:S(2)}, u32[]{:S(2)}) collective-permute-start(bf16[4,1,16,256]{3,2,1,0:T(8,128)(2,1)S(1)} %get-tuple-element.205), channel_id=1, source_target_pairs={{32,0},{64,32},{96,64},{33,1},{65,33},{97,65},{34,2},{66,34},{98,6... | collective-permute-start | bytes 98312 | tf_op jit(solution)/shard_map/ppermute | solution.py:24
  13.2 5.2 %collective-permute-start = (bf16[4,1,16,256]{3,2,1,0:T(8,128)(2,1)S(1)}, bf16[4,1,16,256]{3,2,1,0:T(8,128)(2,1)S(1)}, u32[]{:S(2)}, u32[]{:S(2)}) collective-permute-start(bf16[4,1,16,256]{3,2,1,0:T(8,128)(2,1)S(1)} %get-tuple-element.206), channel_id=1, source_target_pairs={{0,32},{32,64},{64,96},{1,33},{33,65},{65,97},{2,34},{34,66},{66,9... | collective-permute-start | bytes 98312 | tf_op jit(solution)/shard_map/ppermute | solution.py:21
  19.5 9.8 %collective-permute-start.2 = (bf16[4,10,4,256]{3,2,1,0:T(4,128)(2,1)S(1)}, bf16[4,10,4,256]{3,2,1,0:T(4,128)(2,1)S(1)}, u32[]{:S(2)}, u32[]{:S(2)}) collective-permute-start(bf16[4,10,4,256]{3,2,1,0:T(4,128)(2,1)S(1)} %get-tuple-element.201), channel_id=1, source_target_pairs={{0,1},{1,2},{2,3},{3,4},{4,5},{5,6},{6,7},{7,8},{8,9},{9,10},{10,1... | collective-permute-start | bytes 245768 | tf_op jit(solution)/shard_map/ppermute | solution.py:21
  20.6 8.7 %collective-permute-start.3 = (bf16[4,10,4,256]{3,2,1,0:T(4,128)(2,1)S(1)}, bf16[4,10,4,256]{3,2,1,0:T(4,128)(2,1)S(1)}, u32[]{:S(2)}, u32[]{:S(2)}) collective-permute-start(bf16[4,10,4,256]{3,2,1,0:T(4,128)(2,1)S(1)} %get-tuple-element.202), channel_id=1, source_target_pairs={{1,0},{2,1},{3,2},{4,3},{5,4},{6,5},{7,6},{8,7},{9,8},{10,9},{11,1... | collective-permute-start | bytes 245768 | tf_op jit(solution)/shard_map/ppermute | solution.py:24
  57.7 3.5 %copy-start.2 = (bf16[4,8,16,256]{3,2,1,0:T(8,128)(2,1)S(1)}, bf16[4,8,16,256]{3,2,1,0:T(8,128)(2,1)}, u32[]{:S(2)}) copy-start(bf16[4,8,16,256]{3,2,1,0:T(8,128)(2,1)} %param.10) | copy-start | bytes 786436
  57.7 3.5 %copy-start.3 = (bf16[4,8,16,256]{3,2,1,0:T(8,128)(2,1)S(1)}, bf16[4,8,16,256]{3,2,1,0:T(8,128)(2,1)}, u32[]{:S(2)}) copy-start(bf16[4,8,16,256]{3,2,1,0:T(8,128)(2,1)} %param.11) | copy-start | bytes 786436
  61.3 1.8 copy-start.1
  63.1 5.2 %collective-permute-start.4 = (bf16[4,1,16,256]{3,2,1,0:T(8,128)(2,1)S(1)}, bf16[4,1,16,256]{3,2,1,0:T(8,128)(2,1)S(1)}, u32[]{:S(2)}, u32[]{:S(2)}) collective-permute-start(bf16[4,1,16,256]{3,2,1,0:T(8,128)(2,1)S(1)} %get-tuple-element.203), channel_id=1, source_target_pairs={{0,32},{32,64},{64,96},{1,33},{33,65},{65,97},{2,34},{34,66},{66,9... | collective-permute-start | bytes 98312 | tf_op jit(solution)/shard_map/ppermute | solution.py:21
  65.9 5.2 %collective-permute-start.5 = (bf16[4,1,16,256]{3,2,1,0:T(8,128)(2,1)S(1)}, bf16[4,1,16,256]{3,2,1,0:T(8,128)(2,1)S(1)}, u32[]{:S(2)}, u32[]{:S(2)}) collective-permute-start(bf16[4,1,16,256]{3,2,1,0:T(8,128)(2,1)S(1)} %get-tuple-element.204), channel_id=1, source_target_pairs={{32,0},{64,32},{96,64},{33,1},{65,33},{97,65},{34,2},{66,34},{98,6... | collective-permute-start | bytes 98312 | tf_op jit(solution)/shard_map/ppermute | solution.py:24
  71.2 9.5 %collective-permute-start.6 = (bf16[4,10,4,256]{3,2,1,0:T(4,128)(2,1)S(1)}, bf16[4,10,4,256]{3,2,1,0:T(4,128)(2,1)S(1)}, u32[]{:S(2)}, u32[]{:S(2)}) collective-permute-start(bf16[4,10,4,256]{3,2,1,0:T(4,128)(2,1)S(1)} %get-tuple-element.199), channel_id=1, source_target_pairs={{0,1},{1,2},{2,3},{3,4},{4,5},{5,6},{6,7},{7,8},{8,9},{9,10},{10,1... | collective-permute-start | bytes 245768 | tf_op jit(solution)/shard_map/ppermute | solution.py:21
  71.3 9.4 %collective-permute-start.7 = (bf16[4,10,4,256]{3,2,1,0:T(4,128)(2,1)S(1)}, bf16[4,10,4,256]{3,2,1,0:T(4,128)(2,1)S(1)}, u32[]{:S(2)}, u32[]{:S(2)}) collective-permute-start(bf16[4,10,4,256]{3,2,1,0:T(4,128)(2,1)S(1)} %get-tuple-element.200), channel_id=1, source_target_pairs={{1,0},{2,1},{3,2},{4,3},{5,4},{6,5},{7,6},{8,7},{9,8},{10,9},{11,1... | collective-permute-start | bytes 245768 | tf_op jit(solution)/shard_map/ppermute | solution.py:24
Sparse Core Ops, SparseCore 0:
  80.8 256.4 all-reduce.1
where the time goes:
time: 347 us; the launch traced here: 346 us
  waiting for transfers between devices  229 us (66%)
  other arithmetic  53.4 us (15%)
  starting transfers between devices  24.9 us (7%)
  between operations  14.3 us (4%)
  local copies, waits for them, and re-layouts  14 us (4%)
  matrix products  10.5 us (3%)
    psum x1, waiting for transfers between devices, shards(): summed_grad = lax.psum(local_grad, ('ens', 'lat', 'lon'))  224 us
    dynamic_update_slice x8, other arithmetic, spread_forward(): return lax.map(single, padded)  47.4 us
    ppermute x4, starting transfers between devices, extended(): lax.ppermute(lax.slice_in_dim(block, 0, width, axis=dim), axis, backward)  18.9 us
  transfers between devices with their start and end apart: 9, of which 3 were waited for; matrix products, arithmetic and copies ran while one was open for 12% of the time, Pallas kernels for 0%

commit v1 on v0

--- a/solution.py
+++ b/solution.py
@@ -102,6 +102,66 @@
 
 def apply_spread(kernel, padded, coefficients):
     return kernel(padded, coefficients, H)
+
+
+CORES = 2
+YS = 4
+ZS = 8
+XS = 4
+
+
+def core_swap():
+    return [(i, i ^ 1) for i in range(4)]
+
+
+def y_shift(step):
+    return [(y * ZS + z, ((y + step) % YS) * ZS + z) for y in range(YS) for z in range(ZS)]
+
+
+def x_shift(step):
+    return [(i, (i + CORES * step) % (XS * CORES)) for i in range(XS * CORES)]
+
+
+def reduce_gradient(local_grad):
+    half = C // CORES
+    rows = C // YS
+    core = lax.rem(lax.axis_index("lat"), CORES)
+    x_index = lax.axis_index("ens") * 2 + lax.axis_index("lat") // CORES
+    y_index = lax.axis_index("lon") // ZS
+    halves = local_grad.reshape(K, C, CORES, half).transpose(2, 1, 0, 3).reshape(CORES, C, K * half)
+    mine = lax.dynamic_index_in_dim(halves, core, 0, keepdims=False)
+    other = lax.dynamic_index_in_dim(halves, 1 - core, 0, keepdims=False)
+    got = lax.ppermute(other.astype(jnp.bfloat16), "lat", core_swap())
+    blocks = (mine + got.astype(jnp.float32)).reshape(YS, rows, K * half)
+    total = lax.dynamic_index_in_dim(blocks, y_index, 0, keepdims=False)
+    for step in range(1, YS):
+        sent = lax.dynamic_index_in_dim(
+            blocks, lax.rem(y_index + step, YS), 0, keepdims=False
+        ).astype(jnp.bfloat16)
+        total = total + lax.ppermute(sent, "lon", y_shift(step)).astype(jnp.float32)
+    groups = [[y * ZS + z for z in range(ZS)] for y in range(YS)]
+    shares = lax.all_to_all(
+        total.astype(jnp.bfloat16).reshape(ZS, rows // ZS, K * half),
+        "lon",
+        0,
+        0,
+        axis_index_groups=groups,
+        tiled=True,
+    )
+    share = jnp.sum(shares.astype(jnp.float32), axis=0).astype(jnp.bfloat16)
+    held = [share] + [
+        lax.ppermute(share, ("ens", "lat"), x_shift(step)) for step in range(1, XS)
+    ]
+    held = jnp.stack(held).astype(jnp.float32)
+    total = jnp.zeros(share.shape, jnp.float32)
+    for source in range(XS):
+        total = total + lax.dynamic_index_in_dim(
+            held, lax.rem(x_index - source + XS, XS), 0, keepdims=False
+        )
+    other = lax.ppermute(total, "lat", core_swap())
+    low = jnp.where(core == 0, total, other).reshape(-1, K, half)
+    high = jnp.where(core == 0, other, total).reshape(-1, K, half)
+    return jnp.concatenate([low, high], axis=2).transpose(1, 0, 2)
 
 
 def shards(members_in, out_grad, weight, basis_blocks, cycle_block, half_width):
@@ -131,11 +191,7 @@
         feature_rows, grad_mixed, (((0,), (0,)), ((), ())), preferred_element_type=jnp.float32
     )
     local_grad = (local_grad * (1.0 / math.sqrt(cell_count))).reshape(K, C, C)
-    share_size = channels // lax.axis_size("lon")
-    summed_grad = lax.psum(local_grad, ("ens", "lat", "lon"))
-    weight_grad = lax.dynamic_slice_in_dim(
-        summed_grad, lax.axis_index("lon") * share_size, share_size, 1
-    )
+    weight_grad = reduce_gradient(local_grad)
     padded_grad = extend(grad_mixed.reshape(members, lat_rows, lon_cols, channels))
     back = apply_spread(spread_adjoint, padded_grad, wide_coef)
     branch_rows = lax.dot_general(

time: 347 us -> 139 us (0.40)
  waiting for transfers between devices: 229 us -> 6.56 us
  starting transfers between devices: 24.9 us -> 40.3 us
  between operations: 14.3 us -> 1.02 us
  local copies, waits for them, and re-layouts: 14 us -> 22.2 us
  other arithmetic: 53.4 us -> 58.5 us
    psum x1 -> x0, waiting for transfers between devices: 224 us -> none  [shards(): summed_grad = lax.psum(local_grad, ('ens', 'lat', 'lon'))]
    ppermute x0 -> x8, starting transfers between devices: none -> 7.91 us  [the longest x3 4.6 us: reduce_gradient(): lax.ppermute(share, ('ens', 'lat'), x_shift(step))]
    ppermute x4, starting transfers between devices: 5.92 us -> 13.1 us  [extended(): lax.ppermute(lax.slice_in_dim(block, block.shape[dim] - width, None, axis...]
    another operation x2 -> x4, local copies, waits for them, and re-layouts: 4.84 us -> 11.3 us  [the longest x2 6.47 us: reduce_gradient(): local_grad.reshape(K, C, CORES, half).transpose(2, 1, 0, 3)]
    all_to_all x0 -> x1, starting transfers between devices: none -> 5.71 us  [reduce_gradient(): lax.all_to_all(total.astype(jnp.bfloat16).reshape(ZS, rows // ZS, K * hal...]
    ppermute x4, starting transfers between devices: 18.9 us -> 13.7 us  [extended(): lax.ppermute(lax.slice_in_dim(block, 0, width, axis=dim), axis, backward)]
  transfers between devices with their start and end apart: 9 -> 17, of which waited for: 3 -> 4; matrix products, arithmetic and copies ran while one was open for 12% -> 30% of each run, Pallas kernels for 0% -> 0%
where the time goes in v1:
time: 139 us
  other arithmetic  58.5 us (42%)
  starting transfers between devices  40.3 us (29%)
  local copies, waits for them, and re-layouts  22.2 us (16%)
  matrix products  9.74 us (7%)
  waiting for transfers between devices  6.56 us (5%)
    dynamic_update_slice x8, other arithmetic, spread_forward(): return lax.map(single, padded)  47.8 us
    ppermute x4, starting transfers between devices, extended(): lax.ppermute(lax.slice_in_dim(block, 0, width, axis=dim), axis, backward)  13.7 us
    ppermute x4, starting transfers between devices, extended(): lax.ppermute(lax.slice_in_dim(block, block.shape[dim] - width, None, axis...  13.1 us
    another operation x2, local copies, waits for them, and re-layouts, reduce_gradient(): local_grad.reshape(K, C, CORES, half).transpose(2, 1, 0, 3)  6.47 us
    unnamed x16, local copies, waits for them, and re-layouts  6.12 us
    all_to_all x1, starting transfers between devices, reduce_gradient(): lax.all_to_all(total.astype(jnp.bfloat16).reshape(ZS, rows // ZS, K * hal...  5.71 us
    another operation x2, local copies, waits for them, and re-layouts  4.87 us
    ppermute x3, starting transfers between devices, reduce_gradient(): lax.ppermute(share, ('ens', 'lat'), x_shift(step))  4.6 us
  transfers between devices with their start and end apart: 17, of which 4 were waited for; matrix products, arithmetic and copies ran while one was open for 30% of the time, Pallas kernels for 0%

profile of v1, /device:TPU:1, one launch (start us, length us, event | category | flops | bytes accessed | tf_op | source)
XLA Modules:
  0.0 138.7 jit_solution(15387348573393791700)
XLA Ops:
  1.5 4.5 %collective-permute-start = (bf16[4,1,16,256]{3,2,1,0:T(8,128)(2,1)S(1)}, bf16[4,1,16,256]{3,2,1,0:T(8,128)(2,1)S(1)}, u32[]{:S(2)}, u32[]{:S(2)}) collective-permute-start(bf16[4,1,16,256]{3,2,1,0:T(8,128)(2,1)S(1)} %get-tuple-element.217), channel_id=1, source_target_pairs={{0,32},{32,64},{64,96},{1,33},{33,65},{65,97},{2,34},{34,66},{66,9... | collective-permute-start | bytes 98312 | tf_op jit(solution)/shard_map/ppermute | solution.py:21
  14.0 6.5 %collective-permute-start.3 = (bf16[4,10,4,256]{3,2,1,0:T(4,128)(2,1)S(1)}, bf16[4,10,4,256]{3,2,1,0:T(4,128)(2,1)S(1)}, u32[]{:S(2)}, u32[]{:S(2)}) collective-permute-start(bf16[4,10,4,256]{3,2,1,0:T(4,128)(2,1)S(1)} %get-tuple-element.213), channel_id=1, source_target_pairs={{1,0},{2,1},{3,2},{4,3},{5,4},{6,5},{7,6},{8,7},{9,8},{10,9},{11,1... | collective-permute-start | bytes 245768 | tf_op jit(solution)/shard_map/ppermute | solution.py:24
  22.5 2.4 %broadcast.883.clone = bf16[4,8,16,9,256]{4,3,2,1,0:T(8,128)(2,1)} broadcast(bf16[]{:T(256)} %constant.113.clone.1), dimensions={} | broadcast | bytes 2359298 | tf_op jit(solution)/shard_map/broadcast.10
  25.0 25.8 %while.20 = (s32[]{:T(128)}, bf16[4,8,16,9,256]{4,3,2,1,0:T(8,128)(2,1)}, f32[8,9,3,9]{1,0,3,2:T(8,128)S(1)}, bf16[4,10,24,256]{3,2,1,0:T(8,128)(2,1)S(1)}, s32[]{:T(128)}) while((s32[]{:T(128)}, bf16[4,8,16,9,256]{4,3,2,1,0:T(8,128)(2,1)}, f32[8,9,3,9]{1,0,3,2:T(8,128)S(1)}, bf16[4,10,24,256]{3,2,1,0:T(8,128)(2,1)S(1)}, s32[]{:T(128)}) %tuple.167), condition=%wide.region_3.4_spmd, body=%wide.region_2.3_spmd.sunk | while | flops 16809984 | bytes 10165601 | solution.py:78
  25.5 6.0 %fusion.47 = bf16[4,8,16,9,256]{4,3,2,1,0:T(8,128)(2,1)} fusion(bf16[4,8,16,9,256]{4,3,2,1,0:T(8,128)(2,1)} %get-tuple-element.492, s32[]{:T(128)} %get-tuple-element.491, f32[8,16,256]{2,1,0:T(8,128)S(1)} %get-tuple-element.374, f32[8,9]{1,0:T(8,128)S(1)} %get-tuple-element.375, f32[8,16,256]{2,1,0:T(8,128)S(1)} %get-tuple-element.376, ...), kind=kLoop, calls=%fused_computation.1.clone.1 | loop fusion | flops 15925248 | bytes 4595808 | tf_op jit(solution)/shard_map/while/body/jit(dynamic_update_index_in_dim)/dynamic_update_slice | solution.py:78
  31.9 6.0 %fusion.47 = bf16[4,8,16,9,256]{4,3,2,1,0:T(8,128)(2,1)} fusion(bf16[4,8,16,9,256]{4,3,2,1,0:T(8,128)(2,1)} %get-tuple-element.492, s32[]{:T(128)} %get-tuple-element.491, f32[8,16,256]{2,1,0:T(8,128)S(1)} %get-tuple-element.374, f32[8,9]{1,0:T(8,128)S(1)} %get-tuple-element.375, f32[8,16,256]{2,1,0:T(8,128)S(1)} %get-tuple-element.376, ...), kind=kLoop, calls=%fused_computation.1.clone.1 | loop fusion | flops 15925248 | bytes 4595808 | tf_op jit(solution)/shard_map/while/body/jit(dynamic_update_index_in_dim)/dynamic_update_slice | solution.py:78
  38.4 6.0 %fusion.47 = bf16[4,8,16,9,256]{4,3,2,1,0:T(8,128)(2,1)} fusion(bf16[4,8,16,9,256]{4,3,2,1,0:T(8,128)(2,1)} %get-tuple-element.492, s32[]{:T(128)} %get-tuple-element.491, f32[8,16,256]{2,1,0:T(8,128)S(1)} %get-tuple-element.374, f32[8,9]{1,0:T(8,128)S(1)} %get-tuple-element.375, f32[8,16,256]{2,1,0:T(8,128)S(1)} %get-tuple-element.376, ...), kind=kLoop, calls=%fused_computation.1.clone.1 | loop fusion | flops 15925248 | bytes 4595808 | tf_op jit(solution)/shard_map/while/body/jit(dynamic_update_index_in_dim)/dynamic_update_slice | solution.py:78
  44.9 6.0 %fusion.47 = bf16[4,8,16,9,256]{4,3,2,1,0:T(8,128)(2,1)} fusion(bf16[4,8,16,9,256]{4,3,2,1,0:T(8,128)(2,1)} %get-tuple-element.492, s32[]{:T(128)} %get-tuple-element.491, f32[8,16,256]{2,1,0:T(8,128)S(1)} %get-tuple-element.374, f32[8,9]{1,0:T(8,128)S(1)} %get-tuple-element.375, f32[8,16,256]{2,1,0:T(8,128)S(1)} %get-tuple-element.376, ...), kind=kLoop, calls=%fused_computation.1.clone.1 | loop fusion | flops 15925248 | bytes 4595808 | tf_op jit(solution)/shard_map/while/body/jit(dynamic_update_index_in_dim)/dynamic_update_slice | solution.py:78
  50.8 3.5 %copy.39 = bf16[64,8,9,256]{3,1,2,0:T(8,128)(2,1)S(1)} copy(bf16[64,8,9,256]{3,2,1,0:T(8,128)(2,1)} %bitcast.91) | data formatting | bytes 4718592
  56.2 3.2 %convolution_multiply_fusion = f32[2304,256]{1,0:T(8,128)} fusion(bf16[512,2304]{1,0:T(8,128)(2,1)S(1)} %bitcast.203, bf16[512,256]{1,0:T(8,128)(2,1)} %get-tuple-element.208), kind=kOutput, calls=%fused_computation.114 | convolution fusion | flops 604569600 | bytes 4980736 | tf_op jit(solution)/shard_map/dot_general | solution.py:190
  59.4 2.9 %reshape_reshape.3 = f32[9,256,2,128]{3,2,1,0:T(2,128)S(1)} reshape(f32[2304,256]{1,0:T(8,128)} %convolution_multiply_fusion) | data formatting | bytes 4718592 | tf_op jit(solution)/shard_map/reshape;reshape | solution.py:131
  62.3 3.6 %copy.36 = f32[9,256,2,128]{1,3,0,2:T(8,128)} copy(f32[9,256,2,128]{3,2,1,0:T(2,128)S(1)} %reshape_reshape.3) | data formatting | bytes 4718592 | tf_op jit(solution)/shard_map/reshape;reshape | solution.py:131
  73.9 5.3 %collective-permute-start.4 = (bf16[4,1,16,256]{3,2,1,0:T(8,128)(2,1)S(1)}, bf16[4,1,16,256]{3,2,1,0:T(8,128)(2,1)S(1)}, u32[]{:S(2)}, u32[]{:S(2)}) collective-permute-start(bf16[4,1,16,256]{3,2,1,0:T(8,128)(2,1)S(1)} %get-tuple-element.214), channel_id=1, source_target_pairs={{0,32},{32,64},{64,96},{1,33},{33,65},{65,97},{2,34},{34,66},{66,9... | collective-permute-start | bytes 98312 | tf_op jit(solution)/shard_map/ppermute | solution.py:21
  82.4 5.7 %all-to-all-start = ((bf16[8,8,1152]{2,1,0:T(8,128)(2,1)}), bf16[8,8,1152]{2,1,0:T(8,128)(2,1)S(1)}, u32[]{:S(2)}, u32[]{:S(2)}) async-start(bf16[8,8,1152]{2,1,0:T(8,128)(2,1)} %fusion.31), calls=%async_computation | async-start | bytes 294912 | tf_op jit(solution)/shard_map/all_to_all | solution.py:143
  90.7 3.3 %collective-permute-start.7 = (bf16[4,10,4,256]{3,2,1,0:T(4,128)(2,1)S(1)}, bf16[4,10,4,256]{3,2,1,0:T(4,128)(2,1)S(1)}, u32[]{:S(2)}, u32[]{:S(2)}) collective-permute-start(bf16[4,10,4,256]{3,2,1,0:T(4,128)(2,1)S(1)} %get-tuple-element.211), channel_id=1, source_target_pairs={{1,0},{2,1},{3,2},{4,3},{5,4},{6,5},{7,6},{8,7},{9,8},{10,9},{11,1... | collective-permute-start | bytes 245768 | tf_op jit(solution)/shard_map/ppermute | solution.py:24
  94.5 3.6 %collective-permute-done.6 = bf16[4,10,4,256]{3,2,1,0:T(4,128)(2,1)S(1)} collective-permute-done((bf16[4,10,4,256]{3,2,1,0:T(4,128)(2,1)S(1)}, bf16[4,10,4,256]{3,2,1,0:T(4,128)(2,1)S(1)}, u32[]{:S(2)}, u32[]{:S(2)}) %collective-permute-start.6) | collective-permute-done | bytes 81952 | tf_op jit(solution)/shard_map/ppermute | solution.py:21
  100.2 2.5 %collective-permute-start.13 = (bf16[8,1152]{1,0:T(8,128)(2,1)S(1)}, bf16[8,1152]{1,0:T(8,128)(2,1)S(1)}, u32[]{:S(2)}, u32[]{:S(2)}) collective-permute-start(bf16[8,1152]{1,0:T(8,128)(2,1)S(1)} %reduce_sum.32), channel_id=1, source_target_pairs={{0,128},{32,160},{64,192},{96,224},{128,0},{160,32},{192,64},{224,... | collective-permute-start | bytes 55304 | tf_op jit(solution)/shard_map/ppermute | solution.py:153
  104.0 2.4 %broadcast.883 = bf16[4,8,16,9,256]{4,3,2,1,0:T(8,128)(2,1)} broadcast(bf16[]{:T(256)} %constant.113.clone.1), dimensions={} | broadcast | bytes 2359298 | tf_op jit(solution)/shard_map/broadcast.10
  106.4 25.8 %while.21 = (s32[]{:T(128)}, bf16[4,8,16,9,256]{4,3,2,1,0:T(8,128)(2,1)}, f32[10,9,3,9]{1,0,3,2:T(8,128)S(1)}, bf16[4,10,24,256]{3,2,1,0:T(8,128)(2,1)S(1)}, s32[]{:T(128)}) while((s32[]{:T(128)}, bf16[4,8,16,9,256]{4,3,2,1,0:T(8,128)(2,1)}, f32[10,9,3,9]{1,0,3,2:T(8,128)S(1)}, bf16[4,10,24,256]{3,2,1,0:T(8,128)(2,1)S(1)}, s32[]{:T(128)}) %tuple.170), condition=%wide.region_5.6_spmd, body=%wide.region_4.5_spmd.sunk | while | flops 16809984 | bytes 10165601 | solution.py:100
  106.9 6.0 %fusion.48 = bf16[4,8,16,9,256]{4,3,2,1,0:T(8,128)(2,1)} fusion(bf16[4,8,16,9,256]{4,3,2,1,0:T(8,128)(2,1)} %get-tuple-element.507, s32[]{:T(128)} %get-tuple-element.506, f32[8,16,256]{2,1,0:T(8,128)S(1)} %get-tuple-element.432, f32[8,9]{1,0:T(8,128)S(1)} %get-tuple-element.433, f32[8,16,256]{2,1,0:T(8,128)S(1)} %get-tuple-element.434, ...), kind=kLoop, calls=%fused_computation.58.clone.1 | loop fusion | flops 15925248 | bytes 4595808 | tf_op jit(solution)/shard_map/while/body/jit(dynamic_update_index_in_dim)/dynamic_update_slice | solution.py:78
  113.4 6.0 %fusion.48 = bf16[4,8,16,9,256]{4,3,2,1,0:T(8,128)(2,1)} fusion(bf16[4,8,16,9,256]{4,3,2,1,0:T(8,128)(2,1)} %get-tuple-element.507, s32[]{:T(128)} %get-tuple-element.506, f32[8,16,256]{2,1,0:T(8,128)S(1)} %get-tuple-element.432, f32[8,9]{1,0:T(8,128)S(1)} %get-tuple-element.433, f32[8,16,256]{2,1,0:T(8,128)S(1)} %get-tuple-element.434, ...), kind=kLoop, calls=%fused_computation.58.clone.1 | loop fusion | flops 15925248 | bytes 4595808 | tf_op jit(solution)/shard_map/while/body/jit(dynamic_update_index_in_dim)/dynamic_update_slice | solution.py:78
  119.8 6.0 %fusion.48 = bf16[4,8,16,9,256]{4,3,2,1,0:T(8,128)(2,1)} fusion(bf16[4,8,16,9,256]{4,3,2,1,0:T(8,128)(2,1)} %get-tuple-element.507, s32[]{:T(128)} %get-tuple-element.506, f32[8,16,256]{2,1,0:T(8,128)S(1)} %get-tuple-element.432, f32[8,9]{1,0:T(8,128)S(1)} %get-tuple-element.433, f32[8,16,256]{2,1,0:T(8,128)S(1)} %get-tuple-element.434, ...), kind=kLoop, calls=%fused_computation.58.clone.1 | loop fusion | flops 15925248 | bytes 4595808 | tf_op jit(solution)/shard_map/while/body/jit(dynamic_update_index_in_dim)/dynamic_update_slice | solution.py:78
  126.3 6.0 %fusion.48 = bf16[4,8,16,9,256]{4,3,2,1,0:T(8,128)(2,1)} fusion(bf16[4,8,16,9,256]{4,3,2,1,0:T(8,128)(2,1)} %get-tuple-element.507, s32[]{:T(128)} %get-tuple-element.506, f32[8,16,256]{2,1,0:T(8,128)S(1)} %get-tuple-element.432, f32[8,9]{1,0:T(8,128)S(1)} %get-tuple-element.433, f32[8,16,256]{2,1,0:T(8,128)S(1)} %get-tuple-element.434, ...), kind=kLoop, calls=%fused_computation.58.clone.1 | loop fusion | flops 15925248 | bytes 4595808 | tf_op jit(solution)/shard_map/while/body/jit(dynamic_update_index_in_dim)/dynamic_update_slice | solution.py:78
  133.6 4.4 %fusion.10 = bf16[512,256]{1,0:T(8,128)(2,1)} fusion(bf16[9,256,256]{2,1,0:T(8,128)(2,1)S(1)} %copy-done, bf16[512,9,256]{2,1,0:T(8,128)(2,1)} %bitcast.65, bf16[512,256]{1,0:T(8,128)(2,1)S(1)} %bitcast.209), kind=kOutput, calls=%fused_computation.119 | convolution fusion | flops 604372992 | bytes 4063232 | tf_op jit(solution)/shard_map/dot_general | solution.py:197
  (113 shorter events, 35.8 us)
Async XLA Ops:
  0.6 53.7 %copy-start = (bf16[9,256,256]{2,1,0:T(8,128)(2,1)S(1)}, bf16[9,256,256]{2,1,0:T(8,128)(2,1)}, u32[]{:S(2)}) copy-start(bf16[9,256,256]{2,1,0:T(8,128)(2,1)} %param.12) | copy-start | bytes 3538948
  1.5 9.7 %collective-permute-start = (bf16[4,1,16,256]{3,2,1,0:T(8,128)(2,1)S(1)}, bf16[4,1,16,256]{3,2,1,0:T(8,128)(2,1)S(1)}, u32[]{:S(2)}, u32[]{:S(2)}) collective-permute-start(bf16[4,1,16,256]{3,2,1,0:T(8,128)(2,1)S(1)} %get-tuple-element.217), channel_id=1, source_target_pairs={{0,32},{32,64},{64,96},{1,33},{33,65},{65,97},{2,34},{34,66},{66,9... | collective-permute-start | bytes 98312 | tf_op jit(solution)/shard_map/ppermute | solution.py:21
  6.0 6.2 %collective-permute-start.1 = (bf16[4,1,16,256]{3,2,1,0:T(8,128)(2,1)S(1)}, bf16[4,1,16,256]{3,2,1,0:T(8,128)(2,1)S(1)}, u32[]{:S(2)}, u32[]{:S(2)}) collective-permute-start(bf16[4,1,16,256]{3,2,1,0:T(8,128)(2,1)S(1)} %get-tuple-element.216), channel_id=1, source_target_pairs={{32,0},{64,32},{96,64},{33,1},{65,33},{97,65},{34,2},{66,34},{98,6... | collective-permute-start | bytes 98312 | tf_op jit(solution)/shard_map/ppermute | solution.py:24
  12.3 9.9 %collective-permute-start.2 = (bf16[4,10,4,256]{3,2,1,0:T(4,128)(2,1)S(1)}, bf16[4,10,4,256]{3,2,1,0:T(4,128)(2,1)S(1)}, u32[]{:S(2)}, u32[]{:S(2)}) collective-permute-start(bf16[4,10,4,256]{3,2,1,0:T(4,128)(2,1)S(1)} %get-tuple-element.212), channel_id=1, source_target_pairs={{0,1},{1,2},{2,3},{3,4},{4,5},{5,6},{6,7},{7,8},{8,9},{9,10},{10,1... | collective-permute-start | bytes 245768 | tf_op jit(solution)/shard_map/ppermute | solution.py:21
  14.0 8.2 %collective-permute-start.3 = (bf16[4,10,4,256]{3,2,1,0:T(4,128)(2,1)S(1)}, bf16[4,10,4,256]{3,2,1,0:T(4,128)(2,1)S(1)}, u32[]{:S(2)}, u32[]{:S(2)}) collective-permute-start(bf16[4,10,4,256]{3,2,1,0:T(4,128)(2,1)S(1)} %get-tuple-element.213), channel_id=1, source_target_pairs={{1,0},{2,1},{3,2},{4,3},{5,4},{6,5},{7,6},{8,7},{9,8},{10,9},{11,1... | collective-permute-start | bytes 245768 | tf_op jit(solution)/shard_map/ppermute | solution.py:24
  20.8 0.7 copy-start.1
  50.8 3.5 %copy-start.3 = (bf16[4,8,16,256]{3,2,1,0:T(8,128)(2,1)S(1)}, bf16[4,8,16,256]{3,2,1,0:T(8,128)(2,1)}, u32[]{:S(2)}) copy-start(bf16[4,8,16,256]{3,2,1,0:T(8,128)(2,1)} %param.10) | copy-start | bytes 786436
  50.8 3.5 %copy-start.4 = (bf16[4,8,16,256]{3,2,1,0:T(8,128)(2,1)S(1)}, bf16[4,8,16,256]{3,2,1,0:T(8,128)(2,1)}, u32[]{:S(2)}) copy-start(bf16[4,8,16,256]{3,2,1,0:T(8,128)(2,1)} %param.11) | copy-start | bytes 786436
  67.2 2.1 %collective-permute-start.8 = (bf16[256,1152]{0,1:T(8,128)(2,1)S(1)}, bf16[256,1152]{0,1:T(8,128)(2,1)S(1)}, u32[]{:S(2)}, u32[]{:S(2)}) collective-permute-start(bf16[256,1152]{0,1:T(8,128)(2,1)S(1)} %fusion.13), channel_id=1, source_target_pairs={{0,32},{32,0},{64,96},{96,64},{1,33},{33,1},{65,97},{97,65},{2,34}... | collective-permute-start | bytes 1769480 | tf_op jit(solution)/shard_map/ppermute | solution.py:134
  71.1 23.0 %copy-start.2 = (f32[10,9,3,9]{3,0,2,1:T(8,128)S(1)}, f32[10,9,3,9]{3,0,2,1:T(8,128)}, u32[]{:S(2)}) copy-start(f32[10,9,3,9]{3,0,2,1:T(8,128)} %copy-done.1) | copy-start | bytes 29164
  71.2 10.0 %collective-permute-start.10 = (bf16[64,1152]{1,0:T(8,128)(2,1)S(1)}, bf16[64,1152]{1,0:T(8,128)(2,1)S(1)}, u32[]{:S(2)}, u32[]{:S(2)}) collective-permute-start(bf16[64,1152]{1,0:T(8,128)(2,1)S(1)} %get-tuple-element.207), channel_id=1, source_target_pairs={{0,16},{1,17},{2,18},{3,19},{4,20},{5,21},{6,22},{7,23},{8,24},{9,... | collective-permute-start | bytes 442376 | tf_op jit(solution)/shard_map/ppermute | solution.py:141
  71.6 9.5 %collective-permute-start.11 = (bf16[64,1152]{1,0:T(8,128)(2,1)S(1)}, bf16[64,1152]{1,0:T(8,128)(2,1)S(1)}, u32[]{:S(2)}, u32[]{:S(2)}) collective-permute-start(bf16[64,1152]{1,0:T(8,128)(2,1)S(1)} %get-tuple-element.206), channel_id=1, source_target_pairs={{0,24},{1,25},{2,26},{3,27},{4,28},{5,29},{6,30},{7,31},{8,0},{9,1... | collective-permute-start | bytes 442376 | tf_op jit(solution)/shard_map/ppermute | solution.py:141
  72.4 9.3 %collective-permute-start.9 = (bf16[64,1152]{1,0:T(8,128)(2,1)S(1)}, bf16[64,1152]{1,0:T(8,128)(2,1)S(1)}, u32[]{:S(2)}, u32[]{:S(2)}) collective-permute-start(bf16[64,1152]{1,0:T(8,128)(2,1)S(1)} %get-tuple-element.205), channel_id=1, source_target_pairs={{0,8},{1,9},{2,10},{3,11},{4,12},{5,13},{6,14},{7,15},{8,16},{9,17... | collective-permute-start | bytes 442376 | tf_op jit(solution)/shard_map/ppermute | solution.py:141
  73.9 14.3 %collective-permute-start.4 = (bf16[4,1,16,256]{3,2,1,0:T(8,128)(2,1)S(1)}, bf16[4,1,16,256]{3,2,1,0:T(8,128)(2,1)S(1)}, u32[]{:S(2)}, u32[]{:S(2)}) collective-permute-start(bf16[4,1,16,256]{3,2,1,0:T(8,128)(2,1)S(1)} %get-tuple-element.214), channel_id=1, source_target_pairs={{0,32},{32,64},{64,96},{1,33},{33,65},{65,97},{2,34},{34,66},{66,9... | collective-permute-start | bytes 98312 | tf_op jit(solution)/shard_map/ppermute | solution.py:21
  79.2 8.9 %collective-permute-start.5 = (bf16[4,1,16,256]{3,2,1,0:T(8,128)(2,1)S(1)}, bf16[4,1,16,256]{3,2,1,0:T(8,128)(2,1)S(1)}, u32[]{:S(2)}, u32[]{:S(2)}) collective-permute-start(bf16[4,1,16,256]{3,2,1,0:T(8,128)(2,1)S(1)} %get-tuple-element.215), channel_id=1, source_target_pairs={{32,0},{64,32},{96,64},{33,1},{65,33},{97,65},{34,2},{66,34},{98,6... | collective-permute-start | bytes 98312 | tf_op jit(solution)/shard_map/ppermute | solution.py:24
  82.4 16.9 %all-to-all-start = ((bf16[8,8,1152]{2,1,0:T(8,128)(2,1)}), bf16[8,8,1152]{2,1,0:T(8,128)(2,1)S(1)}, u32[]{:S(2)}, u32[]{:S(2)}) async-start(bf16[8,8,1152]{2,1,0:T(8,128)(2,1)} %fusion.31), calls=%async_computation | async-start | bytes 294912 | tf_op jit(solution)/shard_map/all_to_all | solution.py:143
  89.2 8.9 %collective-permute-start.6 = (bf16[4,10,4,256]{3,2,1,0:T(4,128)(2,1)S(1)}, bf16[4,10,4,256]{3,2,1,0:T(4,128)(2,1)S(1)}, u32[]{:S(2)}, u32[]{:S(2)}) collective-permute-start(bf16[4,10,4,256]{3,2,1,0:T(4,128)(2,1)S(1)} %get-tuple-element.210), channel_id=1, source_target_pairs={{0,1},{1,2},{2,3},{3,4},{4,5},{5,6},{6,7},{7,8},{8,9},{9,10},{10,1... | collective-permute-start | bytes 245768 | tf_op jit(solution)/shard_map/ppermute | solution.py:21
  90.7 7.3 %collective-permute-start.7 = (bf16[4,10,4,256]{3,2,1,0:T(4,128)(2,1)S(1)}, bf16[4,10,4,256]{3,2,1,0:T(4,128)(2,1)S(1)}, u32[]{:S(2)}, u32[]{:S(2)}) collective-permute-start(bf16[4,10,4,256]{3,2,1,0:T(4,128)(2,1)S(1)} %get-tuple-element.211), channel_id=1, source_target_pairs={{1,0},{2,1},{3,2},{4,3},{5,4},{6,5},{7,6},{8,7},{9,8},{10,9},{11,1... | collective-permute-start | bytes 245768 | tf_op jit(solution)/shard_map/ppermute | solution.py:24
  99.4 32.9 %collective-permute-start.12 = (bf16[8,1152]{1,0:T(8,128)(2,1)S(1)}, bf16[8,1152]{1,0:T(8,128)(2,1)S(1)}, u32[]{:S(2)}, u32[]{:S(2)}) collective-permute-start(bf16[8,1152]{1,0:T(8,128)(2,1)S(1)} %reduce_sum.32), channel_id=1, source_target_pairs={{0,64},{32,96},{64,128},{96,160},{128,192},{160,224},{192,0},{224,... | collective-permute-start | bytes 55304 | tf_op jit(solution)/shard_map/ppermute | solution.py:153
  100.2 32.1 %collective-permute-start.13 = (bf16[8,1152]{1,0:T(8,128)(2,1)S(1)}, bf16[8,1152]{1,0:T(8,128)(2,1)S(1)}, u32[]{:S(2)}, u32[]{:S(2)}) collective-permute-start(bf16[8,1152]{1,0:T(8,128)(2,1)S(1)} %reduce_sum.32), channel_id=1, source_target_pairs={{0,128},{32,160},{64,192},{96,224},{128,0},{160,32},{192,64},{224,... | collective-permute-start | bytes 55304 | tf_op jit(solution)/shard_map/ppermute | solution.py:153
  102.6 29.6 %collective-permute-start.14 = (bf16[8,1152]{1,0:T(8,128)(2,1)S(1)}, bf16[8,1152]{1,0:T(8,128)(2,1)S(1)}, u32[]{:S(2)}, u32[]{:S(2)}) collective-permute-start(bf16[8,1152]{1,0:T(8,128)(2,1)S(1)} %reduce_sum.32), channel_id=1, source_target_pairs={{0,192},{32,224},{64,0},{96,32},{128,64},{160,96},{192,128},{224,1... | collective-permute-start | bytes 55304 | tf_op jit(solution)/shard_map/ppermute | solution.py:153
  106.4 27.2 %copy-start.5 = (bf16[4,8,16,256]{3,2,1,0:T(8,128)(2,1)S(1)}, bf16[4,8,16,256]{3,2,1,0:T(8,128)(2,1)}, u32[]{:S(2)}) copy-start(bf16[4,8,16,256]{3,2,1,0:T(8,128)(2,1)} %param.11) | copy-start | bytes 786436
  132.3 5.7 %collective-permute-start.15 = (f32[8,1152]{1,0:T(8,128)S(1)}, f32[8,1152]{1,0:T(8,128)S(1)}, u32[]{:S(2)}, u32[]{:S(2)}) collective-permute-start(f32[8,1152]{1,0:T(8,128)S(1)} %add_bitcast_fusion), channel_id=1, source_target_pairs={{0,32},{32,0},{64,96},{96,64},{1,33},{33,1},{65,97},{97,65},{2,34}... | collective-permute-start | bytes 110600 | tf_op jit(solution)/shard_map/ppermute | solution.py:161

commit v2 on v0

v2 whole, which is shorter than its diff:
```python
import functools
import math

import jax
import jax.numpy as jnp
from jax import lax
from jax.experimental import pallas as pl
from jax.experimental.pallas import tpu as pltpu
from jax.sharding import PartitionSpec as P

C = 256
K = 9
R = 1
H = 4
TAPS = 2 * H + 1

CORES = 2
YS = 4
ZS = 8
XS = 4

M = 4
ROWS = 8
COLS = 16
WIDE = COLS + 4 * H
MID = COLS + 2 * H
X_ROWS = ROWS + 4 * R
G_ROWS = ROWS + 2 * R
G_PAD = G_ROWS * MID + 32
BF = jnp.bfloat16
F32 = jnp.float32


def core_swap():
    return [(i, i ^ 1) for i in range(4)]


def y_shift(step):
    return [(y * ZS + z, ((y + step) % YS) * ZS + z) for y in range(YS) for z in range(ZS)]


def fold_kernel(y, mine, got, own, *sent):
    rows = C // YS
    for step in range(YS):
        at = pl.multiple_of(lax.rem(y[0] + step, YS) * rows, rows)
        total = mine[pl.ds(at, rows), :].astype(F32) + got[pl.ds(at, rows), :].astype(F32)
        if step == 0:
            own[...] = total
        else:
            sent[step - 1][...] = total.astype(BF)


def join_kernel(own, one, two, three, out):
    total = own[...] + one[...].astype(F32) + two[...].astype(F32) + three[...].astype(F32)
    out[...] = total.reshape(out.shape).astype(BF)


def share_kernel(shares, out):
    total = shares[0].astype(F32)
    for z in range(1, ZS):
        total = total + shares[z].astype(F32)
    for copy in range(XS * CORES):
        out[copy] = total.astype(BF)


def place_kernel(shares, out):
    half = C // CORES
    for core in range(CORES):
        total = shares[core].astype(F32)
        for x in range(1, XS):
            total = total + shares[x * CORES + core].astype(F32)
        for k in range(K):
            out[k, :, core * half : (core + 1) * half] = total[:, k * half : (k + 1) * half]


def table_kernel(cycles, widths, first, basis, x, near, far, x_turned):
    lane = lax.broadcasted_iota(jnp.int32, (1, 128), 1)
    total = cycles.shape[0]
    blocks = []
    reach = []
    for row in range(G_ROWS):
        cycle = jnp.clip(first[0] + (row - R), 0, total - 1)
        blocks.append(cycles[cycle])
        reach.append([widths[r, cycle] for r in range(3)])
    for p in range(G_ROWS // 2):
        bases = []
        for row in (2 * p, 2 * p + 1):
            limit = jnp.where(
                lane < 32, reach[row][0], jnp.where(lane < 64, reach[row][1], reach[row][2])
            )
            inside = jnp.abs((lane & 31) - H) <= limit
            base = jnp.where(inside, basis[blocks[row], :, 0:128], 0.0)
            bases.append(pltpu.roll(base, 32, 1) if row % 2 else base)
        for k in range(K):
            bands = [
                pltpu.roll(
                    jnp.broadcast_to(base[k : k + 1], (MID, 128)), 0, 1, stride=1, stride_axis=0
                )
                for base in bases
            ]
            near[p, k] = jnp.concatenate(bands, axis=0).astype(BF)
    for row in range(ROWS):
        base = jnp.zeros((K, 128), F32)
        for t in range(3):
            place = lane - MID * t
            inside = (place >= 0) & (place < TAPS) & (jnp.abs(place - H) <= reach[row + t][2 - t])
            base = base + jnp.where(inside, basis[blocks[row + t], :, 128:256], 0.0)
        if row % 2:
            base = pltpu.roll(base, MID, 1)
        for k in range(K):
            band = pltpu.roll(
                jnp.broadcast_to(base[k : k + 1], (COLS, 128)), 0, 1, stride=1, stride_axis=0
            )
            far[row // 2, k, COLS * (row % 2) : COLS * (row % 2) + COLS] = band.astype(BF)
    for m in range(M):
        flat = x[m].reshape(ROWS * COLS, C).astype(F32)
        x_turned[:, m * ROWS * COLS : (m + 1) * ROWS * COLS] = flat.T.astype(BF)


def side_kernel(x_in, grad_in, left, right, x, grad, sems):
    copies = [
        pltpu.make_async_copy(x_in, x, sems.at[0]),
        pltpu.make_async_copy(grad_in, grad, sems.at[1]),
    ]
    for copy in copies:
        copy.start()
    copies[0].wait()

    def x_member(m, carry):
        for r in range(ROWS):
            row = x[m, r].astype(F32)
            left[m, r] = row[0:8].astype(BF)
            right[m, r] = row[8:16].astype(BF)
        return carry

    lax.fori_loop(0, M, x_member, 0)
    copies[1].wait()

    def g_member(m, carry):
        for q in range(ROWS // 2):
            one = grad[m, 2 * q].astype(F32)
            two = grad[m, 2 * q + 1].astype(F32)
            left[m, ROWS + q] = jnp.concatenate([one[0:4], two[0:4]], axis=0).astype(BF)
            right[m, ROWS + q] = jnp.concatenate([one[12:16], two[12:16]], axis=0).astype(BF)
        return carry

    lax.fori_loop(0, M, g_member, 0)


def rim_rows(x, grad, left_x, right_x, left_g, right_g, at, out):
    def member(m, carry):
        for r in range(2):
            row = x[m, r].astype(F32)
            out[m, 4 * r] = left_x[m, r]
            out[m, 4 * r + 1] = row[0:8].astype(BF)
            out[m, 4 * r + 2] = row[8:16].astype(BF)
            out[m, 4 * r + 3] = right_x[m, r]
        before = left_g[m, 0].astype(F32)[at : at + 4]
        after = right_g[m, 0].astype(F32)[at : at + 4]
        line = jnp.concatenate([before, grad[m, 0].astype(F32), after], axis=0).astype(BF)
        for t in range(3):
            out[m, 8 + t] = line[8 * t : 8 * t + 8]
        return carry

    lax.fori_loop(0, M, member, 0)


def rim_kernel(*refs):
    rim_rows(*refs[0:6], 4, refs[12])
    rim_rows(*refs[6:12], 0, refs[13])


def adjoint_rows(far, grads, back):
    def member(m, carry):
        for p in range(ROWS // 2):
            spread = jnp.dot(
                far[p].reshape(K * 32, 128),
                grads[m, 2 * MID * p : 2 * MID * p + 128],
                preferred_element_type=F32,
            )
            start = pl.multiple_of(m * ROWS * COLS + 32 * p, 32)
            for k in range(K):
                back[pl.ds(start, 32), k * C : (k + 1) * C] = spread[32 * k : 32 * k + 32].astype(BF)
        return carry

    lax.fori_loop(0, M, member, 0)


def main_kernel(
    scale, core, x, x_turned, out_grad, weight, near, far, top_in, bottom_in, left_in, right_in,
    result, grads, mine, other,
    wide, cotangent, features, mixed, back, top, bottom, left, right, sems,
):
    copies = [
        pltpu.make_async_copy(source, target, sems.at[n])
        for n, (source, target) in enumerate(
            ((left_in, left), (right_in, right), (top_in, top), (bottom_in, bottom))
        )
    ]
    for copy in copies:
        copy.start()
    for copy in copies:
        copy.wait()

    def gather(m, carry):
        for r in range(2):
            for at, rim in ((r, top), (X_ROWS - 2 + r, bottom)):
                row = jnp.concatenate([rim[m, 4 * r + t].astype(F32) for t in range(4)], axis=0)
                wide[m, WIDE * at : WIDE * at + WIDE] = row.astype(BF)
        for at, rim in ((0, top), (G_ROWS - 1, bottom)):
            cotangent[m, MID * at : MID * at + MID] = jnp.concatenate(
                [rim[m, 8 + t].astype(F32) for t in range(3)], axis=0
            )
        for r in range(ROWS):
            row = jnp.concatenate(
                [left[m, r].astype(F32), x[m, r].astype(F32), right[m, r].astype(F32)], axis=0
            )
            wide[m, WIDE * (r + 2) : WIDE * (r + 2) + WIDE] = row.astype(BF)
            at = 4 * (r % 2)
            before = left[m, ROWS + r // 2].astype(F32)[at : at + 4]
            after = right[m, ROWS + r // 2].astype(F32)[at : at + 4]
            cotangent[m, MID * (r + 1) : MID * (r + 1) + MID] = jnp.concatenate(
                [before, out_grad[m, r].astype(F32), after], axis=0
            )
        for p in range(G_ROWS // 2):
            spread = jnp.dot(
                near[p].reshape(K * 2 * MID, 128),
                wide[m, 2 * WIDE * p : 2 * WIDE * p + 128],
                preferred_element_type=F32,
            )
            start = pl.multiple_of(m * G_ROWS * MID + 2 * MID * p, 16)
            for k in range(K):
                features[pl.ds(start, 2 * MID), k * C : (k + 1) * C] = spread[
                    2 * MID * k : 2 * MID * k + 2 * MID
                ].astype(BF)
        return carry

    lax.fori_loop(0, M, gather, 0)
    mixed[...] = jnp.dot(features[...], weight[...], preferred_element_type=F32).reshape(
        M, G_ROWS * MID, C
    )
    slope = math.sqrt(2.0 / math.pi)

    def activate(m, carry):
        for p in range(G_ROWS // 2):
            v = mixed[m, 2 * MID * p : 2 * MID * p + 2 * MID]
            square = v * v
            t = jnp.tanh(slope * v * (1.0 + 0.044715 * square))
            half = 0.5 * (1.0 + t)
            rise = half + 0.5 * v * (1.0 - t * t) * (slope * (1.0 + 3 * 0.044715 * square))
            grad = cotangent[m, 2 * MID * p : 2 * MID * p + 2 * MID] * rise
            grads[m, 2 * MID * p : 2 * MID * p + 2 * MID] = grad.astype(BF)
            act = v * half
            for part in range(2):
                r = 2 * p + part - R
                if 0 <= r < ROWS:
                    own = act[MID * part + H : MID * part + H + COLS]
                    result[m, r] = (x[m, r].astype(F32) + own).astype(BF)
        grads[m, G_ROWS * MID : G_PAD] = jnp.zeros((G_PAD - G_ROWS * MID, C), BF)
        return carry

    lax.fori_loop(0, M, activate, 0)
    adjoint_rows(far, grads, back)
    first = core[0] == 0
    for k in range(K):
        part = scale * jnp.dot(
            x_turned[...], back[:, k * C : (k + 1) * C], preferred_element_type=F32
        )
        low = part[:, 0:128]
        high = part[:, 128:256]
        mine[:, 128 * k : 128 * k + 128] = jnp.where(first, low, high).astype(BF)
        other[:, 128 * k : 128 * k + 128] = jnp.where(first, high, low).astype(BF)


def tail_kernel(grads, out_grad, weight, far, tie, in_grad, tied, back):
    adjoint_rows(far, grads, back)
    total = out_grad[...].reshape(M * ROWS * COLS, C).astype(F32)
    for k in range(K):
        total = total + lax.dot_general(
            back[:, k * C : (k + 1) * C],
            weight[k],
            (((1,), (1,)), ((), ())),
            preferred_element_type=F32,
        )
    in_grad[...] = total.reshape(M, ROWS, COLS, C).astype(BF)


VM = pl.BlockSpec(memory_space=pltpu.VMEM)
SM = pl.BlockSpec(memory_space=pltpu.SMEM)
KEPT = pl.BlockSpec(memory_space=pl.ANY)
FAR = pl.BlockSpec(memory_space=pltpu.HBM)


def call(kernel, ins, outs, args, name, scratch=(), mib=8, flops=0, moved=1 << 20, tie=None, sems=0):
    aliases = {}
    out_specs = [VM] * len(outs)
    outs = [jax.ShapeDtypeStruct(*o) for o in outs]
    if tie is not None:
        aliases = {len(args): len(outs)}
        ins = ins + [KEPT]
        args = args + (tie,)
        out_specs = out_specs + [KEPT]
        outs = outs + [jax.ShapeDtypeStruct(tie.shape, tie.dtype)]
    return pl.pallas_call(
        kernel,
        out_shape=outs,
        in_specs=ins,
        out_specs=out_specs,
        scratch_shapes=[pltpu.VMEM(*s) for s in scratch]
        + [pltpu.SemaphoreType.DMA((sems,))] * (sems > 0),
        input_output_aliases=aliases,
        cost_estimate=pl.CostEstimate(flops=flops, bytes_accessed=moved, transcendentals=0),
        compiler_params=pltpu.CompilerParams(vmem_limit_bytes=mib << 20),
        name=name,
    )(*args)


def edge(rows, block, width):
    return pl.BlockSpec((M, rows, width, C), lambda i: (0, block, 0, 0))


def send_sides(x, out_grad):
    shape = (M, ROWS + ROWS // 2, 8, C)
    to_left, to_right = call(
        side_kernel,
        [FAR] * 2,
        [(shape, BF)] * 2,
        (x, out_grad),
        "side",
        scratch=[(x.shape, BF)] * 2,
        sems=2,
    )
    count = lax.axis_size("lon")
    left = lax.ppermute(to_right, "lon", [(i, (i + 1) % count) for i in range(count)])
    right = lax.ppermute(to_left, "lon", [((i + 1) % count, i) for i in range(count)])
    return left, right


def send_rims(x, out_grad, left, right):
    shape = (M, 11, 8, C)
    whole = pl.BlockSpec(shape, lambda i: (0, 0, 0, 0))
    ins = []
    for x_at, g_at in ((ROWS // 2 - 1, ROWS - 1), (0, 0)):
        ins += [edge(2, x_at, COLS), edge(1, g_at, COLS)]
        ins += [edge(2, x_at, 8)] * 2 + [edge(1, ROWS + g_at // 2, 8)] * 2
    up, down = pl.pallas_call(
        rim_kernel,
        grid=(1,),
        out_shape=[jax.ShapeDtypeStruct(shape, BF)] * 2,
        in_specs=ins,
        out_specs=[whole] * 2,
        cost_estimate=pl.CostEstimate(flops=0, bytes_accessed=1 << 18, transcendentals=0),
        compiler_params=pltpu.CompilerParams(vmem_limit_bytes=6 << 20),
        name="rim",
    )(*((x, out_grad, left, right, left, right) * 2))
    count = lax.axis_size("lat")
    top = lax.ppermute(up, "lat", [(i, i + 1) for i in range(count - 1)])
    bottom = lax.ppermute(down, "lat", [(i + 1, i) for i in range(count - 1)])
    return top, bottom


def reduce_gradient(mine, other, behind):
    half = K * C // CORES
    rows = C // YS
    share_rows = rows // ZS
    y_index = (lax.axis_index("lon") // ZS).reshape(1)
    got = lax.ppermute(other, "lat", core_swap())
    own, *sent = call(
        fold_kernel,
        [SM, VM, VM],
        [((rows, half), F32)] + [((rows, half), BF)] * 3,
        (y_index, mine, got),
        "fold",
    )
    parts = [lax.ppermute(sent[step - 1], "lon", y_shift(step)) for step in range(1, YS)]
    extra, own = behind(own)
    (joined,) = call(
        join_kernel, [VM] * 4, [((ZS, share_rows, half), BF)], (own, *parts), "join"
    )
    groups = [[y * ZS + z for z in range(ZS)] for y in range(YS)]
    shares = lax.all_to_all(joined, "lon", 0, 0, axis_index_groups=groups, tiled=True)
    (share,) = call(
        share_kernel, [VM], [((XS * CORES, share_rows, half), BF)], (shares,), "share"
    )
    shares = lax.all_to_all(share, ("ens", "lat"), 0, 0, tiled=True)
    (weight_grad,) = call(place_kernel, [VM], [((K, share_rows, C), F32)], (shares,), "place")
    return weight_grad, extra


def shards(members_in, out_grad, weight, basis_blocks, cycle_block, half_width):
    lat = lax.axis_index("lat")
    left, right = send_sides(members_in, out_grad)
    blocks = basis_blocks.shape[0]
    basis = jnp.pad(basis_blocks, ((0, 0), (0, 0), (0, 0), (0, 32 - TAPS))).reshape(blocks, K, 96)
    flipped = jnp.pad(
        basis_blocks[:, :, ::-1, ::-1], ((0, 0), (0, 0), (0, 0), (0, MID - TAPS))
    ).reshape(blocks, K, 72)
    gap = jnp.zeros((blocks, K, 32), F32)
    basis = jnp.concatenate([basis, gap, flipped, gap, gap[:, :, :24]], axis=2)

    near, far, x_turned = call(
        table_kernel,
        [SM] * 3 + [VM] * 2,
        [
            ((G_ROWS // 2, K, 2 * MID, 128), BF),
            ((ROWS // 2, K, 32, 128), BF),
            ((C, M * ROWS * COLS), BF),
        ],
        (cycle_block, half_width.T, (lat * ROWS).reshape(1), basis, members_in),
        "table",
        flops=1 << 24,
        moved=3 << 20,
    )
    top, bottom = send_rims(members_in, out_grad, left, right)
    cell_count = (
        M * lax.axis_size("ens") * ROWS * lax.axis_size("lat") * COLS * lax.axis_size("lon")
    )
    half_shape = (C, K * C // CORES)
    result, grads, mine, other = call(
        functools.partial(main_kernel, 1.0 / math.sqrt(cell_count)),
        [SM] + [VM] * 6 + [FAR] * 4,
        [
            (members_in.shape, BF),
            ((M, G_PAD, C), BF),
            (half_shape, BF),
            (half_shape, BF),
        ],
        (
            lax.rem(lat, CORES).reshape(1),
            members_in,
            x_turned,
            out_grad,
            weight.reshape(K * C, C),
            near,
            far,
            top,
            bottom,
            left,
            right,
        ),
        "main",
        scratch=[
            ((M, X_ROWS * WIDE, C), BF),
            ((M, G_ROWS * MID, C), F32),
            ((M * G_ROWS * MID, K * C), BF),
            ((M, G_ROWS * MID, C), F32),
            ((M * ROWS * COLS, K * C), BF),
            (top.shape, BF),
            (bottom.shape, BF),
            (left.shape, BF),
            (right.shape, BF),
        ],
        sems=4,
        mib=32,
        flops=5 << 30,
        moved=8 << 20,
    )

    def tail(tie):
        return call(
            tail_kernel,
            [VM] * 4,
            [(members_in.shape, BF)],
            (grads, out_grad, weight, far),
            "tail",
            scratch=[((M * ROWS * COLS, K * C), BF)],
            mib=16,
            flops=2 << 30,
            moved=4 << 20,
            tie=tie,
        )

    weight_grad, in_grad = reduce_gradient(mine, other, tail)
    return (result, in_grad, weight_grad)


def solution(mesh):
    return jax.shard_map(
        shards,
        mesh=mesh,
        in_specs=(P("ens", "lat", "lon", None), P("ens", "lat", "lon", None), P(), P(), P(), P()),
        out_specs=(
            P("ens", "lat", "lon", None),
            P("ens", "lat", "lon", None),
            P(None, "lon", None),
        ),
        check_vma=False,
    )
```

time: 347 us -> 74.7 us (0.22)
  waiting for transfers between devices: 229 us -> 13.5 us
  other arithmetic: 53.4 us -> 0 us
  blocking collectives: 0 us -> 24.1 us
  between operations: 14.3 us -> 0.87 us
  Pallas kernels: 0 us -> 12.8 us
  matrix products: 10.5 us -> 0 us
  local copies, waits for them, and re-layouts: 14 us -> 5.18 us
  starting transfers between devices: 24.9 us -> 17.9 us
    psum x1 -> x0, waiting for transfers between devices: 224 us -> none  [shards(): summed_grad = lax.psum(local_grad, ('ens', 'lat', 'lon'))]
    dynamic_update_slice x8 -> x0, other arithmetic: 47.4 us -> none  [spread_forward(): return lax.map(single, padded)]
    all_to_all x0 -> x2, blocking collectives: none -> 24.1 us  [the longest x1 12.4 us: reduce_gradient(): lax.all_to_all(joined, 'lon', 0, 0, axis_index_groups=groups, tiled=True)]
    pallas_call x0 -> x9, Pallas kernels: none -> 12.8 us  [the longest x8 12.7 us: call(): pl.pallas_call(kernel, out_shape=outs, in_specs=ins, out_specs=out_specs,...]
    dot_general x4 -> x0, matrix products: 10.5 us -> none  [the longest x1 4.4 us: shards(): lax.dot_general(back.reshape(-1, K, C), weight, (((1, 2), (0, 2)), ((), (...]
    ppermute x8, waiting for transfers between devices: 4.53 us -> 13.5 us  [the longest x3 4.54 us: reduce_gradient(): lax.ppermute(sent[step - 1], 'lon', y_shift(step))]
    ppermute x8, starting transfers between devices: 24.8 us -> 17.9 us  [the longest x1 6.49 us: send_sides(): lax.ppermute(to_left, 'lon', [((i + 1) % count, i) for i in range(count)])]
    another operation x2 -> x0, local copies, waits for them, and re-layouts: 4.84 us -> none
  transfers between devices with their start and end apart: 9 -> 8, of which waited for: 3 -> 5; matrix products, arithmetic and copies ran while one was open for 12% -> 1% of each run, Pallas kernels for 0% -> 6%
where the time goes in v2:
time: 74.7 us; the launch traced here: 74.4 us
  blocking collectives  24.1 us (32%)
  starting transfers between devices  17.9 us (24%)
  waiting for transfers between devices  13.5 us (18%)
  Pallas kernels  12.8 us (17%)
  local copies, waits for them, and re-layouts  5.18 us (7%)
  between operations  0.87 us (1%)
    pallas_call x8, Pallas kernels, call(): pl.pallas_call(kernel, out_shape=outs, in_specs=ins, out_specs=out_specs,...  12.7 us
    all_to_all x1, blocking collectives, reduce_gradient(): lax.all_to_all(joined, 'lon', 0, 0, axis_index_groups=groups, tiled=True)  12.4 us
    all_to_all x1, blocking collectives, reduce_gradient(): shares = lax.all_to_all(share, ('ens', 'lat'), 0, 0, tiled=True)  11.7 us
    ppermute x1, starting transfers between devices, send_sides(): lax.ppermute(to_left, 'lon', [((i + 1) % count, i) for i in range(count)])  6.49 us
    unnamed x30, local copies, waits for them, and re-layouts  4.66 us
    ppermute x3, waiting for transfers between devices, reduce_gradient(): lax.ppermute(sent[step - 1], 'lon', y_shift(step))  4.54 us
    ppermute x1, waiting for transfers between devices, send_sides(): lax.ppermute(to_right, 'lon', [(i, (i + 1) % count) for i in range(count)])  4.5 us
    ppermute x1, starting transfers between devices, send_rims(): top = lax.ppermute(up, 'lat', [(i, i + 1) for i in range(count - 1)])  4.26 us
  transfers between devices with their start and end apart: 8, of which 5 were waited for; matrix products, arithmetic and copies ran while one was open for 1% of the time, Pallas kernels for 6%

profile of v2, /device:TPU:1, one launch (start us, length us, event | category | flops | bytes accessed | tf_op | source)
XLA Modules:
  0.0 74.4 jit_solution(4562483624066682594)
XLA Ops:
  0.6 0.9 %copy-done = bf16[4,8,16,256]{3,2,1,0:T(8,128)(2,1)S(1)} copy-done((bf16[4,8,16,256]{3,2,1,0:T(8,128)(2,1)S(1)}, bf16[4,8,16,256]{3,2,1,0:T(8,128)(2,1)}, u32[]{:S(2)}) %copy-start) | copy-done | bytes 262168
  1.6 0.9 %copy-done.2 = bf16[4,8,16,256]{3,2,1,0:T(8,128)(2,1)S(1)} copy-done((bf16[4,8,16,256]{3,2,1,0:T(8,128)(2,1)S(1)}, bf16[4,8,16,256]{3,2,1,0:T(8,128)(2,1)}, u32[]{:S(2)}) %copy-start.2) | copy-done | bytes 262168
  2.7 2.5 %collective-permute-start = (bf16[4,12,8,256]{3,2,1,0:T(8,128)(2,1)S(1)}, bf16[4,12,8,256]{3,2,1,0:T(8,128)(2,1)S(1)}, u32[]{:S(2)}, u32[]{:S(2)}) collective-permute-start(bf16[4,12,8,256]{3,2,1,0:T(8,128)(2,1)S(1)} %get-tuple-element.23), channel_id=1, source_target_pairs={{0,1},{1,2},{2,3},{3,4},{4,5},{5,6},{6,7},{7,8},{8,9},{9,10},{10,1... | collective-permute-start | bytes 589832 | tf_op jit(solution)/shard_map/ppermute | solution.py:334
  5.2 6.5 %collective-permute-start.1 = (bf16[4,12,8,256]{3,2,1,0:T(8,128)(2,1)S(1)}, bf16[4,12,8,256]{3,2,1,0:T(8,128)(2,1)S(1)}, u32[]{:S(2)}, u32[]{:S(2)}) collective-permute-start(bf16[4,12,8,256]{3,2,1,0:T(8,128)(2,1)S(1)} %get-tuple-element.24), channel_id=1, source_target_pairs={{1,0},{2,1},{3,2},{4,3},{5,4},{6,5},{7,6},{8,7},{9,8},{10,9},{11,1... | collective-permute-start | bytes 589832 | tf_op jit(solution)/shard_map/ppermute | solution.py:335
  11.7 4.5 %collective-permute-done.refs_2_.refs_4_.refs_8_.refs_10_.left_in = bf16[4,12,8,256]{3,2,1,0:T(8,128)(2,1)S(1)} collective-permute-done((bf16[4,12,8,256]{3,2,1,0:T(8,128)(2,1)S(1)}, bf16[4,12,8,256]{3,2,1,0:T(8,128)(2,1)S(1)}, u32[]{:S(2)}, u32[]{:S(2)}) %collective-permute-start) | collective-permute-done | bytes 196640 | tf_op jit(solution)/shard_map/ppermute | solution.py:334
  16.3 4.3 %collective-permute-start.2 = (bf16[4,11,8,256]{3,2,1,0:T(8,128)(2,1)S(1)}, bf16[4,11,8,256]{3,2,1,0:T(8,128)(2,1)S(1)}, u32[]{:S(2)}, u32[]{:S(2)}) collective-permute-start(bf16[4,11,8,256]{3,2,1,0:T(8,128)(2,1)S(1)} %get-tuple-element.25), channel_id=1, source_target_pairs={{0,32},{32,64},{64,96},{1,33},{33,65},{65,97},{2,34},{34,66},{66,9... | collective-permute-start | bytes 540680 | tf_op jit(solution)/shard_map/ppermute | solution.py:357
  20.6 1.9 %collective-permute-start.3 = (bf16[4,11,8,256]{3,2,1,0:T(8,128)(2,1)S(1)}, bf16[4,11,8,256]{3,2,1,0:T(8,128)(2,1)S(1)}, u32[]{:S(2)}, u32[]{:S(2)}) collective-permute-start(bf16[4,11,8,256]{3,2,1,0:T(8,128)(2,1)S(1)} %get-tuple-element.26), channel_id=1, source_target_pairs={{32,0},{64,32},{96,64},{33,1},{65,33},{97,65},{34,2},{66,34},{98,6... | collective-permute-start | bytes 540680 | tf_op jit(solution)/shard_map/ppermute | solution.py:358
  23.2 0.2 copy-done.1
  23.5 1.4 %table.1 = (bf16[5,9,48,128]{3,2,1,0:T(8,128)(2,1)S(1)}, bf16[4,9,32,128]{3,2,1,0:T(8,128)(2,1)S(1)}, bf16[256,512]{1,0:T(8,128)(2,1)S(1)}) custom-call(s32[32]{0:T(128)S(1)} %copy-done.5, s32[3,32]{1,0:T(4,128)S(1)} %bitcast.5, s32[1]{0:T(128)} %bitcast.2.first, f32[8,9,256]{2,1,0:T(8,128)S(1)} %concatenate.3.basis, bf16[4,8,16,256]{3,2,1,0:T(8,128)(2,1)S(1)} %copy-done.1), custom_call_target="tpu_custom_call" | custom-call | flops 16777216 | bytes 3145728 | tf_op jit(solution)/shard_map/table/pallas_call | solution.py:304
  24.9 2.4 %collective-permute-done.3.bottom_in = bf16[4,11,8,256]{3,2,1,0:T(8,128)(2,1)S(1)} collective-permute-done((bf16[4,11,8,256]{3,2,1,0:T(8,128)(2,1)S(1)}, bf16[4,11,8,256]{3,2,1,0:T(8,128)(2,1)S(1)}, u32[]{:S(2)}, u32[]{:S(2)}) %collective-permute-start.3) | collective-permute-done | bytes 180256 | tf_op jit(solution)/shard_map/ppermute | solution.py:358
  27.4 0.7 copy-done.9
  28.1 0.9 %copy-done.10 = bf16[4,11,8,256]{3,2,1,0:T(8,128)(2,1)S(1)} copy-done((bf16[4,11,8,256]{3,2,1,0:T(8,128)(2,1)S(1)}, bf16[4,11,8,256]{3,2,1,0:T(8,128)(2,1)}, u32[]{:S(2)}) %copy-start.10) | copy-done | bytes 180248
  29.0 7.5 %main.1 = (bf16[4,8,16,256]{3,2,1,0:T(8,128)(2,1)}, bf16[4,272,256]{2,1,0:T(8,128)(2,1)S(1)}, bf16[256,1152]{1,0:T(8,128)(2,1)S(1)}, bf16[256,1152]{1,0:T(8,128)(2,1)S(1)}) custom-call(s32[1]{0:T(128)} %bitcast.core, bf16[4,8,16,256]{3,2,1,0:T(8,128)(2,1)S(1)} %copy-done.1, bf16[256,512]{1,0:T(8,128)(2,1)S(1)} %get-tuple-element.20.x_turned, ...), custom_call_target="tpu_custom_call" | custom-call | flops 5368709120 | bytes 8388608 | tf_op jit(solution)/shard_map/main/pallas_call | solution.py:304
  36.5 0.8 %copy-done.11 = bf16[4,272,256]{2,1,0:T(8,128)(2,1)} copy-done((bf16[4,272,256]{2,1,0:T(8,128)(2,1)}, bf16[4,272,256]{2,1,0:T(8,128)(2,1)S(1)}, u32[]{:S(2)}) %copy-start.11) | copy-done | bytes 557080
  37.3 2.0 %collective-permute-done.4.got = bf16[256,1152]{1,0:T(8,128)(2,1)S(1)} collective-permute-done((bf16[256,1152]{1,0:T(8,128)(2,1)S(1)}, bf16[256,1152]{1,0:T(8,128)(2,1)S(1)}, u32[]{:S(2)}, u32[]{:S(2)}) %collective-permute-start.4) | collective-permute-done | bytes 589856 | tf_op jit(solution)/shard_map/ppermute | solution.py:367
  39.3 0.1 fold.1
  39.5 1.6 %collective-permute-start.6 = (bf16[64,1152]{1,0:T(8,128)(2,1)S(1)}, bf16[64,1152]{1,0:T(8,128)(2,1)S(1)}, u32[]{:S(2)}, u32[]{:S(2)}) collective-permute-start(bf16[64,1152]{1,0:T(8,128)(2,1)S(1)} %get-tuple-element.35), channel_id=1, source_target_pairs={{0,16},{1,17},{2,18},{3,19},{4,20},{5,21},{6,22},{7,23},{8,24},{9,... | collective-permute-start | bytes 442376 | tf_op jit(solution)/shard_map/ppermute | solution.py:375
  41.2 1.0 %collective-permute-start.7 = (bf16[64,1152]{1,0:T(8,128)(2,1)S(1)}, bf16[64,1152]{1,0:T(8,128)(2,1)S(1)}, u32[]{:S(2)}, u32[]{:S(2)}) collective-permute-start(bf16[64,1152]{1,0:T(8,128)(2,1)S(1)} %get-tuple-element.36), channel_id=1, source_target_pairs={{0,24},{1,25},{2,26},{3,27},{4,28},{5,29},{6,30},{7,31},{8,0},{9,1... | collective-permute-start | bytes 442376 | tf_op jit(solution)/shard_map/ppermute | solution.py:375
  42.2 2.8 %tail.1 = (bf16[4,8,16,256]{3,2,1,0:T(8,128)(2,1)}, f32[64,1152]{1,0:T(8,128)S(1)}) custom-call(bf16[4,272,256]{2,1,0:T(8,128)(2,1)S(1)} %copy-done.12, bf16[4,8,16,256]{3,2,1,0:T(8,128)(2,1)S(1)} %copy-done.3, bf16[9,256,256]{2,1,0:T(8,128)(2,1)S(1)} %copy-done.6, bf16[4,9,32,128]{3,2,1,0:T(8,128)(2,1)S(1)} %copy-done.8, ...), custom_call_target="tpu_custom_call", output_to_operand_aliasing={{1}: (4, {})} | custom-call | flops 2147483648 | bytes 4194304 | tf_op jit(solution)/shard_map/tail/pallas_call | solution.py:304
  45.0 4.2 %collective-permute-done.5.one = bf16[64,1152]{1,0:T(8,128)(2,1)S(1)} collective-permute-done((bf16[64,1152]{1,0:T(8,128)(2,1)S(1)}, bf16[64,1152]{1,0:T(8,128)(2,1)S(1)}, u32[]{:S(2)}, u32[]{:S(2)}) %collective-permute-start.5) | collective-permute-done | bytes 147488 | tf_op jit(solution)/shard_map/ppermute | solution.py:375
  49.2 0.3 collective-permute-done.7.three
  49.6 12.4 %all_to_all.10.shares = bf16[8,8,1152]{2,1,0:T(8,128)(2,1)S(1)} all-to-all(bf16[8,8,1152]{2,1,0:T(8,128)(2,1)S(1)} %join.1), channel_id=1, replica_groups={{0,1,2,3,4,5,6,7},{8,9,10,11,12,13,14,15},{16,17,18,19,20,21,22,23},{24..., dimensions={0} | all-to-all | bytes 294912 | tf_op jit(solution)/shard_map/all_to_all | solution.py:381
  62.0 11.7 %all_to_all.11.shares = bf16[8,8,1152]{2,1,0:T(8,128)(2,1)S(1)} all-to-all(bf16[8,8,1152]{2,1,0:T(8,128)(2,1)S(1)} %share.1), channel_id=1, replica_groups=mesh['ens'=2,'lat'=4,'lon'=32] {'ens','lat'}, dimensions={0} | all-to-all | bytes 294912 | tf_op jit(solution)/shard_map/all_to_all | solution.py:385
  73.7 0.7 place.1
  (41 shorter events, 1.1 us)
Async XLA Ops:
  0.6 1.0 %copy-start = (bf16[4,8,16,256]{3,2,1,0:T(8,128)(2,1)S(1)}, bf16[4,8,16,256]{3,2,1,0:T(8,128)(2,1)}, u32[]{:S(2)}) copy-start(bf16[4,8,16,256]{3,2,1,0:T(8,128)(2,1)} %x.7) | copy-start | bytes 786436
  1.6 0.9 %copy-start.2 = (bf16[4,8,16,256]{3,2,1,0:T(8,128)(2,1)S(1)}, bf16[4,8,16,256]{3,2,1,0:T(8,128)(2,1)}, u32[]{:S(2)}) copy-start(bf16[4,8,16,256]{3,2,1,0:T(8,128)(2,1)} %out_grad.3) | copy-start | bytes 786436
  2.7 13.5 %collective-permute-start = (bf16[4,12,8,256]{3,2,1,0:T(8,128)(2,1)S(1)}, bf16[4,12,8,256]{3,2,1,0:T(8,128)(2,1)S(1)}, u32[]{:S(2)}, u32[]{:S(2)}) collective-permute-start(bf16[4,12,8,256]{3,2,1,0:T(8,128)(2,1)S(1)} %get-tuple-element.23), channel_id=1, source_target_pairs={{0,1},{1,2},{2,3},{3,4},{4,5},{5,6},{6,7},{7,8},{8,9},{9,10},{10,1... | collective-permute-start | bytes 589832 | tf_op jit(solution)/shard_map/ppermute | solution.py:334
  5.2 17.3 %copy-start.13 = (f32[8,9,3,9]{3,0,2,1:T(8,128)S(1)}, f32[8,9,3,9]{3,0,2,1:T(8,128)}, u32[]{:S(2)}) copy-start(f32[8,9,3,9]{3,0,2,1:T(8,128)} %param.9) | copy-start | bytes 23332
  5.2 11.0 %collective-permute-start.1 = (bf16[4,12,8,256]{3,2,1,0:T(8,128)(2,1)S(1)}, bf16[4,12,8,256]{3,2,1,0:T(8,128)(2,1)S(1)}, u32[]{:S(2)}, u32[]{:S(2)}) collective-permute-start(bf16[4,12,8,256]{3,2,1,0:T(8,128)(2,1)S(1)} %get-tuple-element.24), channel_id=1, source_target_pairs={{1,0},{2,1},{3,2},{4,3},{5,4},{6,5},{7,6},{8,7},{9,8},{10,9},{11,1... | collective-permute-start | bytes 589832 | tf_op jit(solution)/shard_map/ppermute | solution.py:335
  16.3 8.6 %collective-permute-start.2 = (bf16[4,11,8,256]{3,2,1,0:T(8,128)(2,1)S(1)}, bf16[4,11,8,256]{3,2,1,0:T(8,128)(2,1)S(1)}, u32[]{:S(2)}, u32[]{:S(2)}) collective-permute-start(bf16[4,11,8,256]{3,2,1,0:T(8,128)(2,1)S(1)} %get-tuple-element.25), channel_id=1, source_target_pairs={{0,32},{32,64},{64,96},{1,33},{33,65},{65,97},{2,34},{34,66},{66,9... | collective-permute-start | bytes 540680 | tf_op jit(solution)/shard_map/ppermute | solution.py:357
  20.6 6.8 %collective-permute-start.3 = (bf16[4,11,8,256]{3,2,1,0:T(8,128)(2,1)S(1)}, bf16[4,11,8,256]{3,2,1,0:T(8,128)(2,1)S(1)}, u32[]{:S(2)}, u32[]{:S(2)}) collective-permute-start(bf16[4,11,8,256]{3,2,1,0:T(8,128)(2,1)S(1)} %get-tuple-element.26), channel_id=1, source_target_pairs={{32,0},{64,32},{96,64},{33,1},{65,33},{97,65},{34,2},{66,34},{98,6... | collective-permute-start | bytes 540680 | tf_op jit(solution)/shard_map/ppermute | solution.py:358
  22.5 1.0 %copy-start.1 = (bf16[4,8,16,256]{3,2,1,0:T(8,128)(2,1)S(1)}, bf16[4,8,16,256]{3,2,1,0:T(8,128)(2,1)}, u32[]{:S(2)}) copy-start(bf16[4,8,16,256]{3,2,1,0:T(8,128)(2,1)} %x.7) | copy-start | bytes 786436
  22.5 0.9 %copy-start.4 = (s32[32,3]{0,1:T(4,128)S(1)}, s32[32,3]{0,1:T(4,128)}, u32[]{:S(2)}) copy-start(s32[32,3]{0,1:T(4,128)} %param.11) | copy-start | bytes 1156
  22.5 0.9 %copy-start.5 = (s32[32]{0:T(128)S(1)}, s32[32]{0:T(128)}, u32[]{:S(2)}) copy-start(s32[32]{0:T(128)} %cycles.1) | copy-start | bytes 388
  22.7 5.4 %copy-start.3 = (bf16[4,8,16,256]{3,2,1,0:T(8,128)(2,1)S(1)}, bf16[4,8,16,256]{3,2,1,0:T(8,128)(2,1)}, u32[]{:S(2)}) copy-start(bf16[4,8,16,256]{3,2,1,0:T(8,128)(2,1)} %out_grad.3) | copy-start | bytes 786436
  22.7 5.4 %copy-start.6 = (bf16[9,256,256]{2,1,0:T(8,128)(2,1)S(1)}, bf16[9,256,256]{2,1,0:T(8,128)(2,1)}, u32[]{:S(2)}) copy-start(bf16[9,256,256]{2,1,0:T(8,128)(2,1)} %weight.1) | copy-start | bytes 3538948
  24.9 11.6 %copy-start.7 = (bf16[4,9,32,128]{3,2,1,0:T(8,128)(2,1)}, bf16[4,9,32,128]{3,2,1,0:T(8,128)(2,1)S(1)}, u32[]{:S(2)}) copy-start(bf16[4,9,32,128]{3,2,1,0:T(8,128)(2,1)S(1)} %get-tuple-element.22.far) | copy-start | bytes 884740
  27.4 0.7 copy-start.9
  28.1 0.9 %copy-start.10 = (bf16[4,11,8,256]{3,2,1,0:T(8,128)(2,1)S(1)}, bf16[4,11,8,256]{3,2,1,0:T(8,128)(2,1)}, u32[]{:S(2)}) copy-start(bf16[4,11,8,256]{3,2,1,0:T(8,128)(2,1)} %copy-done.9) | copy-start | bytes 540676
  36.5 0.8 %copy-start.11 = (bf16[4,272,256]{2,1,0:T(8,128)(2,1)}, bf16[4,272,256]{2,1,0:T(8,128)(2,1)S(1)}, u32[]{:S(2)}) copy-start(bf16[4,272,256]{2,1,0:T(8,128)(2,1)S(1)} %get-tuple-element.28.grads) | copy-start | bytes 1671172
  37.3 2.0 %collective-permute-start.4 = (bf16[256,1152]{1,0:T(8,128)(2,1)S(1)}, bf16[256,1152]{1,0:T(8,128)(2,1)S(1)}, u32[]{:S(2)}, u32[]{:S(2)}) collective-permute-start(bf16[256,1152]{1,0:T(8,128)(2,1)S(1)} %get-tuple-element.30), channel_id=1, source_target_pairs={{0,32},{32,0},{64,96},{96,64},{1,33},{33,1},{65,97},{97,65},{2,34}... | collective-permute-start | bytes 1769480 | tf_op jit(solution)/shard_map/ppermute | solution.py:367
  37.3 4.9 %copy-start.8 = (bf16[4,9,32,128]{3,2,1,0:T(8,128)(2,1)S(1)}, bf16[4,9,32,128]{3,2,1,0:T(8,128)(2,1)}, u32[]{:S(2)}) copy-start(bf16[4,9,32,128]{3,2,1,0:T(8,128)(2,1)} %copy-done.7) | copy-start | bytes 884740
  37.3 4.9 %copy-start.12 = (bf16[4,272,256]{2,1,0:T(8,128)(2,1)S(1)}, bf16[4,272,256]{2,1,0:T(8,128)(2,1)}, u32[]{:S(2)}) copy-start(bf16[4,272,256]{2,1,0:T(8,128)(2,1)} %copy-done.11) | copy-start | bytes 1671172
  39.4 9.7 %collective-permute-start.5 = (bf16[64,1152]{1,0:T(8,128)(2,1)S(1)}, bf16[64,1152]{1,0:T(8,128)(2,1)S(1)}, u32[]{:S(2)}, u32[]{:S(2)}) collective-permute-start(bf16[64,1152]{1,0:T(8,128)(2,1)S(1)} %get-tuple-element.34), channel_id=1, source_target_pairs={{0,8},{1,9},{2,10},{3,11},{4,12},{5,13},{6,14},{7,15},{8,16},{9,17... | collective-permute-start | bytes 442376 | tf_op jit(solution)/shard_map/ppermute | solution.py:375
  39.5 9.6 %collective-permute-start.6 = (bf16[64,1152]{1,0:T(8,128)(2,1)S(1)}, bf16[64,1152]{1,0:T(8,128)(2,1)S(1)}, u32[]{:S(2)}, u32[]{:S(2)}) collective-permute-start(bf16[64,1152]{1,0:T(8,128)(2,1)S(1)} %get-tuple-element.35), channel_id=1, source_target_pairs={{0,16},{1,17},{2,18},{3,19},{4,20},{5,21},{6,22},{7,23},{8,24},{9,... | collective-permute-start | bytes 442376 | tf_op jit(solution)/shard_map/ppermute | solution.py:375
  41.2 8.3 %collective-permute-start.7 = (bf16[64,1152]{1,0:T(8,128)(2,1)S(1)}, bf16[64,1152]{1,0:T(8,128)(2,1)S(1)}, u32[]{:S(2)}, u32[]{:S(2)}) collective-permute-start(bf16[64,1152]{1,0:T(8,128)(2,1)S(1)} %get-tuple-element.36), channel_id=1, source_target_pairs={{0,24},{1,25},{2,26},{3,27},{4,28},{5,29},{6,30},{7,31},{8,0},{9,1... | collective-permute-start | bytes 442376 | tf_op jit(solution)/shard_map/ppermute | solution.py:375

commit v3 on v2

--- a/solution.py
+++ b/solution.py
@@ -166,8 +166,8 @@
 
 
 def rim_kernel(*refs):
-    rim_rows(*refs[0:6], 4, refs[12])
-    rim_rows(*refs[6:12], 0, refs[13])
+    rim_rows(*refs[0:6], 4, refs[13])
+    rim_rows(*refs[6:12], 0, refs[14])
 
 
 def adjoint_rows(far, grads, back):
@@ -186,80 +186,135 @@
     lax.fori_loop(0, M, member, 0)
 
 
-def main_kernel(
-    scale, core, x, x_turned, out_grad, weight, near, far, top_in, bottom_in, left_in, right_in,
-    result, grads, mine, other,
-    wide, cotangent, features, mixed, back, top, bottom, left, right, sems,
+def full_row(left, middle, right):
+    return jnp.concatenate(
+        [left.astype(F32), middle.astype(F32), right.astype(F32)], axis=0
+    ).astype(BF)
+
+
+def grad_row(left, out_grad, right, m, r):
+    at = 4 * (r % 2)
+    before = left[m, ROWS + r // 2].astype(F32)[at : at + 4]
+    after = right[m, ROWS + r // 2].astype(F32)[at : at + 4]
+    return jnp.concatenate([before, out_grad[m, r].astype(F32), after], axis=0)
+
+
+def spread_pair(near, window, features, start):
+    spread = jnp.dot(
+        near.reshape(K * 2 * MID, 128), window, preferred_element_type=F32
+    )
+    for k in range(K):
+        features[pl.ds(start, 2 * MID), k * C : (k + 1) * C] = spread[
+            2 * MID * k : 2 * MID * k + 2 * MID
+        ].astype(BF)
+
+
+def activate(v, cotangent):
+    slope = math.sqrt(2.0 / math.pi)
+    square = v * v
+    t = jnp.tanh(slope * v * (1.0 + 0.044715 * square))
+    half = 0.5 * (1.0 + t)
+    rise = half + 0.5 * v * (1.0 - t * t) * (slope * (1.0 + 3 * 0.044715 * square))
+    return v * half, (cotangent * rise).astype(BF)
+
+
+def inner_kernel(
+    x, out_grad, near, left, right, weight_in, after,
+    middle, result_out,
+    wide, cotangent, features, mixed, result, weight, sems,
 ):
+    copy = pltpu.make_async_copy(weight_in, weight, sems.at[0])
+    copy.start()
+    pairs = G_ROWS // 2 - 2
+
+    def gather(m, carry):
+        for r in range(ROWS):
+            wide[m, WIDE * r : WIDE * r + WIDE] = full_row(left[m, r], x[m, r], right[m, r])
+        for r in range(1, ROWS - 1):
+            cotangent[m, MID * (r - 1) : MID * r] = grad_row(left, out_grad, right, m, r)
+        for q in range(pairs):
+            start = pl.multiple_of(m * pairs * 2 * MID + 2 * MID * q, 16)
+            spread_pair(near[q + 1], wide[m, 2 * WIDE * q : 2 * WIDE * q + 128], features, start)
+        return carry
+
+    lax.fori_loop(0, M, gather, 0)
+    copy.wait()
+    mixed[...] = jnp.dot(features[...], weight[...], preferred_element_type=F32).reshape(
+        mixed.shape
+    )
+
+    def finish(m, carry):
+        for q in range(pairs):
+            rows = slice(2 * MID * q, 2 * MID * q + 2 * MID)
+            act, grad = activate(mixed[m, rows], cotangent[m, rows])
+            middle[m, rows] = grad
+            for part in range(2):
+                own = act[MID * part + H : MID * part + H + COLS]
+                r = 2 * q + part
+                result[m, r] = (x[m, r + 1].astype(F32) + own).astype(BF)
+        return carry
+
+    lax.fori_loop(0, M, finish, 0)
+    copy = pltpu.make_async_copy(result, result_out.at[:, 1 : ROWS - 1], sems.at[1])
+    copy.start()
+    copy.wait()
+
+
+def outer_kernel(
+    scale, core, x, x_turned, out_grad, near, far, top, bottom, left, right, middle, weight_in,
+    tie, mine, other, grads_out, result_out,
+    wide, cotangent, features, mixed, result, grads, back, weight, sems,
+):
+    copy = pltpu.make_async_copy(weight_in, weight, sems.at[0])
+    copy.start()
+    last = G_ROWS // 2 - 1
+
+    def gather(m, carry):
+        for r in range(2):
+            for at, rim in ((r, top), (6 + r, bottom)):
+                row = jnp.concatenate([rim[m, 4 * r + t].astype(F32) for t in range(4)], axis=0)
+                wide[m, WIDE * at : WIDE * at + WIDE] = row.astype(BF)
+            for at, own in ((2 + r, r), (4 + r, ROWS - 2 + r)):
+                wide[m, WIDE * at : WIDE * at + WIDE] = full_row(
+                    left[m, own], x[m, own], right[m, own]
+                )
+        for at, rim in ((0, top), (3, bottom)):
+            cotangent[m, MID * at : MID * at + MID] = jnp.concatenate(
+                [rim[m, 8 + t].astype(F32) for t in range(3)], axis=0
+            )
+        for at, own in ((1, 0), (2, ROWS - 1)):
+            cotangent[m, MID * at : MID * at + MID] = grad_row(left, out_grad, right, m, own)
+        for q, p in enumerate((0, last)):
+            start = pl.multiple_of(m * 4 * MID + 2 * MID * q, 16)
+            spread_pair(near[p], wide[m, 128 * q : 128 * q + 128], features, start)
+        return carry
+
+    lax.fori_loop(0, M, gather, 0)
+    copy.wait()
+    mixed[...] = jnp.dot(features[...], weight[...], preferred_element_type=F32).reshape(
+        mixed.shape
+    )
+
+    def finish(m, carry):
+        for q, p in enumerate((0, last)):
+            rows = slice(2 * MID * q, 2 * MID * q + 2 * MID)
+            act, grad = activate(mixed[m, rows], cotangent[m, rows])
+            grads[m, 2 * MID * p : 2 * MID * p + 2 * MID] = grad
+            part = 1 - q
+            own = act[MID * part + H : MID * part + H + COLS]
+            result[q, m] = (x[m, (ROWS - 1) * q].astype(F32) + own).astype(BF)
+        grads[m, 2 * MID : 2 * MID * last] = middle[m]
+        grads[m, G_ROWS * MID : G_PAD] = jnp.zeros((G_PAD - G_ROWS * MID, C), BF)
+        return carry
+
+    lax.fori_loop(0, M, finish, 0)
     copies = [
-        pltpu.make_async_copy(source, target, sems.at[n])
-        for n, (source, target) in enumerate(
-            ((left_in, left), (right_in, right), (top_in, top), (bottom_in, bottom))
-        )
+        pltpu.make_async_copy(grads, grads_out, sems.at[1]),
+        pltpu.make_async_copy(result.at[0], result_out.at[:, 0], sems.at[2]),
+        pltpu.make_async_copy(result.at[1], result_out.at[:, ROWS - 1], sems.at[3]),
     ]
     for copy in copies:
         copy.start()
-    for copy in copies:
-        copy.wait()
-
-    def gather(m, carry):
-        for r in range(2):
-            for at, rim in ((r, top), (X_ROWS - 2 + r, bottom)):
-                row = jnp.concatenate([rim[m, 4 * r + t].astype(F32) for t in range(4)], axis=0)
-                wide[m, WIDE * at : WIDE * at + WIDE] = row.astype(BF)
-        for at, rim in ((0, top), (G_ROWS - 1, bottom)):
-            cotangent[m, MID * at : MID * at + MID] = jnp.concatenate(
-                [rim[m, 8 + t].astype(F32) for t in range(3)], axis=0
-            )
-        for r in range(ROWS):
-            row = jnp.concatenate(
-                [left[m, r].astype(F32), x[m, r].astype(F32), right[m, r].astype(F32)], axis=0
-            )
-            wide[m, WIDE * (r + 2) : WIDE * (r + 2) + WIDE] = row.astype(BF)
-            at = 4 * (r % 2)
-            before = left[m, ROWS + r // 2].astype(F32)[at : at + 4]
-            after = right[m, ROWS + r // 2].astype(F32)[at : at + 4]
-            cotangent[m, MID * (r + 1) : MID * (r + 1) + MID] = jnp.concatenate(
-                [before, out_grad[m, r].astype(F32), after], axis=0
-            )
-        for p in range(G_ROWS // 2):
-            spread = jnp.dot(
-                near[p].reshape(K * 2 * MID, 128),
-                wide[m, 2 * WIDE * p : 2 * WIDE * p + 128],
-                preferred_element_type=F32,
-            )
-            start = pl.multiple_of(m * G_ROWS * MID + 2 * MID * p, 16)
-            for k in range(K):
-                features[pl.ds(start, 2 * MID), k * C : (k + 1) * C] = spread[
-                    2 * MID * k : 2 * MID * k + 2 * MID
-                ].astype(BF)
-        return carry
-
-    lax.fori_loop(0, M, gather, 0)
-    mixed[...] = jnp.dot(features[...], weight[...], preferred_element_type=F32).reshape(
-        M, G_ROWS * MID, C
-    )
-    slope = math.sqrt(2.0 / math.pi)
-
-    def activate(m, carry):
-        for p in range(G_ROWS // 2):
-            v = mixed[m, 2 * MID * p : 2 * MID * p + 2 * MID]
-            square = v * v
-            t = jnp.tanh(slope * v * (1.0 + 0.044715 * square))
-            half = 0.5 * (1.0 + t)
-            rise = half + 0.5 * v * (1.0 - t * t) * (slope * (1.0 + 3 * 0.044715 * square))
-            grad = cotangent[m, 2 * MID * p : 2 * MID * p + 2 * MID] * rise
-            grads[m, 2 * MID * p : 2 * MID * p + 2 * MID] = grad.astype(BF)
-            act = v * half
-            for part in range(2):
-                r = 2 * p + part - R
-                if 0 <= r < ROWS:
-                    own = act[MID * part + H : MID * part + H + COLS]
-                    result[m, r] = (x[m, r].astype(F32) + own).astype(BF)
-        grads[m, G_ROWS * MID : G_PAD] = jnp.zeros((G_PAD - G_ROWS * MID, C), BF)
-        return carry
-
-    lax.fori_loop(0, M, activate, 0)
     adjoint_rows(far, grads, back)
     first = core[0] == 0
     for k in range(K):
@@ -270,15 +325,23 @@
         high = part[:, 128:256]
         mine[:, 128 * k : 128 * k + 128] = jnp.where(first, low, high).astype(BF)
         other[:, 128 * k : 128 * k + 128] = jnp.where(first, high, low).astype(BF)
-
-
-def tail_kernel(grads, out_grad, weight, far, tie, in_grad, tied, back):
+    for copy in copies:
+        copy.wait()
+
+
+def tail_kernel(grads_in, out_grad, far, weight_in, tie, in_grad, tied, back, weight, grads, sems):
+    copy = pltpu.make_async_copy(weight_in, weight, sems.at[0])
+    fetch = pltpu.make_async_copy(grads_in, grads, sems.at[1])
+    fetch.start()
+    copy.start()
+    fetch.wait()
     adjoint_rows(far, grads, back)
+    copy.wait()
     total = out_grad[...].reshape(M * ROWS * COLS, C).astype(F32)
     for k in range(K):
         total = total + lax.dot_general(
             back[:, k * C : (k + 1) * C],
-            weight[k],
+            weight[k * C : (k + 1) * C],
             (((1,), (1,)), ((), ())),
             preferred_element_type=F32,
         )
@@ -291,10 +354,16 @@
 FAR = pl.BlockSpec(memory_space=pltpu.HBM)
 
 
-def call(kernel, ins, outs, args, name, scratch=(), mib=8, flops=0, moved=1 << 20, tie=None, sems=0):
+def call(
+    kernel, ins, outs, args, name,
+    scratch=(), mib=8, flops=0, moved=1 << 20, tie=None, sems=0, away=(),
+):
     aliases = {}
     out_specs = [VM] * len(outs)
     outs = [jax.ShapeDtypeStruct(*o) for o in outs]
+    for shape, dtype in away:
+        out_specs = out_specs + [FAR]
+        outs = outs + [pltpu.HBM(shape, dtype)]
     if tie is not None:
         aliases = {len(args): len(outs)}
         ins = ins + [KEPT]
@@ -328,6 +397,7 @@
         (x, out_grad),
         "side",
         scratch=[(x.shape, BF)] * 2,
+        mib=60,
         sems=2,
     )
     count = lax.axis_size("lon")
@@ -336,7 +406,7 @@
     return left, right
 
 
-def send_rims(x, out_grad, left, right):
+def send_rims(x, out_grad, left, right, after):
     shape = (M, 11, 8, C)
     whole = pl.BlockSpec(shape, lambda i: (0, 0, 0, 0))
     ins = []
@@ -347,16 +417,16 @@
         rim_kernel,
         grid=(1,),
         out_shape=[jax.ShapeDtypeStruct(shape, BF)] * 2,
-        in_specs=ins,
+        in_specs=ins + [KEPT],
         out_specs=[whole] * 2,
         cost_estimate=pl.CostEstimate(flops=0, bytes_accessed=1 << 18, transcendentals=0),
         compiler_params=pltpu.CompilerParams(vmem_limit_bytes=6 << 20),
         name="rim",
-    )(*((x, out_grad, left, right, left, right) * 2))
+    )(*((x, out_grad, left, right, left, right) * 2), after)
     count = lax.axis_size("lat")
     top = lax.ppermute(up, "lat", [(i, i + 1) for i in range(count - 1)])
     bottom = lax.ppermute(down, "lat", [(i + 1, i) for i in range(count - 1)])
-    return top, bottom
+    return up, top, bottom
 
 
 def reduce_gradient(mine, other, behind):
@@ -411,60 +481,85 @@
         flops=1 << 24,
         moved=3 << 20,
     )
-    top, bottom = send_rims(members_in, out_grad, left, right)
+    up, top, bottom = send_rims(members_in, out_grad, left, right, far)
+    flat_weight = pltpu.with_memory_space_constraint(weight.reshape(K * C, C), pltpu.HBM)
     cell_count = (
         M * lax.axis_size("ens") * ROWS * lax.axis_size("lat") * COLS * lax.axis_size("lon")
     )
     half_shape = (C, K * C // CORES)
-    result, grads, mine, other = call(
-        functools.partial(main_kernel, 1.0 / math.sqrt(cell_count)),
-        [SM] + [VM] * 6 + [FAR] * 4,
-        [
-            (members_in.shape, BF),
-            ((M, G_PAD, C), BF),
-            (half_shape, BF),
-            (half_shape, BF),
+    inner = (G_ROWS - 4) * MID
+    middle, result = call(
+        inner_kernel,
+        [VM] * 5 + [FAR, KEPT],
+        [((M, inner, C), BF)],
+        (members_in, out_grad, near, left, right, flat_weight, up),
+        "inner",
+        scratch=[
+            ((M, ROWS * WIDE, C), BF),
+            ((M, inner, C), F32),
+            ((M * inner, K * C), BF),
+            ((M, inner, C), F32),
+            ((M, ROWS - 2, COLS, C), BF),
+            (flat_weight.shape, BF),
         ],
+        mib=18,
+        sems=2,
+        flops=3 << 30,
+        moved=4 << 20,
+        away=[(members_in.shape, BF)],
+    )
+    outer = 4 * MID
+    mine, other, grads, result = call(
+        functools.partial(outer_kernel, 1.0 / math.sqrt(cell_count)),
+        [SM] + [VM] * 10 + [FAR],
+        [(half_shape, BF)] * 2,
         (
             lax.rem(lat, CORES).reshape(1),
             members_in,
             x_turned,
             out_grad,
-            weight.reshape(K * C, C),
             near,
             far,
             top,
             bottom,
             left,
             right,
+            middle,
+            flat_weight,
         ),
-        "main",
+        "outer",
         scratch=[
-            ((M, X_ROWS * WIDE, C), BF),
-            ((M, G_ROWS * MID, C), F32),
-            ((M * G_ROWS * MID, K * C), BF),
-            ((M, G_ROWS * MID, C), F32),
+            ((M, 8 * WIDE, C), BF),
+            ((M, outer, C), F32),
+            ((M * outer, K * C), BF),
+            ((M, outer, C), F32),
+            ((2, M, COLS, C), BF),
+            ((M, G_PAD, C), BF),
             ((M * ROWS * COLS, K * C), BF),
-            (top.shape, BF),
-            (bottom.shape, BF),
-            (left.shape, BF),
-            (right.shape, BF),
+            (flat_weight.shape, BF),
         ],
+        mib=18,
         sems=4,
-        mib=32,
-        flops=5 << 30,
-        moved=8 << 20,
+        flops=4 << 30,
+        moved=4 << 20,
+        away=[((M, G_PAD, C), BF)],
+        tie=result,
     )
 
     def tail(tie):
         return call(
             tail_kernel,
-            [VM] * 4,
+            [FAR] + [VM] * 2 + [FAR],
             [(members_in.shape, BF)],
-            (grads, out_grad, weight, far),
+            (grads, out_grad, far, flat_weight),
             "tail",
-            scratch=[((M * ROWS * COLS, K * C), BF)],
-            mib=16,
+            scratch=[
+                ((M * ROWS * COLS, K * C), BF),
+                (flat_weight.shape, BF),
+                (grads.shape, BF),
+            ],
+            sems=2,
+            mib=8,
             flops=2 << 30,
             moved=4 << 20,
             tie=tie,

time: 74.7 us -> 67.7 us (0.906)
  waiting for transfers between devices: 13.5 us -> 7.13 us
  local copies, waits for them, and re-layouts: 5.18 us -> 2.46 us
  Pallas kernels: 12.8 us -> 14.8 us
    ppermute x1, waiting for transfers between devices: 4.5 us -> 0.73 us  [send_sides(): lax.ppermute(to_right, 'lon', [(i, (i + 1) % count) for i in range(count)])]
    unnamed x30 -> x12, local copies, waits for them, and re-layouts: 4.66 us -> 1 us
    ppermute x1, waiting for transfers between devices: 2.45 us -> 0.01 us  [send_rims(): bottom = lax.ppermute(down, 'lat', [(i + 1, i) for i in range(count - 1)])]
    pallas_call x8 -> x9, Pallas kernels: 12.7 us -> 14.7 us  [call(): pl.pallas_call(kernel, out_shape=outs, in_specs=ins, out_specs=out_specs,...]
    ppermute x1, starting transfers between devices: 4.26 us -> 3.02 us  [send_rims(): top = lax.ppermute(up, 'lat', [(i, i + 1) for i in range(count - 1)])]
    ppermute x1, starting transfers between devices: 1.92 us -> 3.16 us  [send_rims(): bottom = lax.ppermute(down, 'lat', [(i + 1, i) for i in range(count - 1)])]
    rev x1, local copies, waits for them, and re-layouts: 0.09 us -> 1.02 us  [shards(): basis_blocks[:, :, ::-1, ::-1]]
  transfers between devices with their start and end apart: 8 -> 8, of which waited for: 5 -> 4; matrix products, arithmetic and copies ran while one was open for 1% -> 4% of each run, Pallas kernels for 6% -> 11%
where the time goes in v3:
time: 67.7 us; the launch traced here: 67.4 us
  blocking collectives  24.1 us (36%)
  starting transfers between devices  18 us (27%)
  Pallas kernels  14.8 us (22%)
  waiting for transfers between devices  7.13 us (11%)
  local copies, waits for them, and re-layouts  2.46 us (4%)
  between operations  0.86 us (1%)
    pallas_call x9, Pallas kernels, call(): pl.pallas_call(kernel, out_shape=outs, in_specs=ins, out_specs=out_specs,...  14.7 us
    all_to_all x1, blocking collectives, reduce_gradient(): lax.all_to_all(joined, 'lon', 0, 0, axis_index_groups=groups, tiled=True)  12.4 us
    all_to_all x1, blocking collectives, reduce_gradient(): shares = lax.all_to_all(share, ('ens', 'lat'), 0, 0, tiled=True)  11.7 us
    ppermute x1, starting transfers between devices, send_sides(): lax.ppermute(to_left, 'lon', [((i + 1) % count, i) for i in range(count)])  6.48 us
    ppermute x3, waiting for transfers between devices, reduce_gradient(): lax.ppermute(sent[step - 1], 'lon', y_shift(step))  4.42 us
    ppermute x1, starting transfers between devices, send_rims(): bottom = lax.ppermute(down, 'lat', [(i + 1, i) for i in range(count - 1)])  3.16 us
    ppermute x1, starting transfers between devices, send_rims(): top = lax.ppermute(up, 'lat', [(i, i + 1) for i in range(count - 1)])  3.02 us
    ppermute x3, starting transfers between devices, reduce_gradient(): lax.ppermute(sent[step - 1], 'lon', y_shift(step))  2.75 us
  transfers between devices with their start and end apart: 8, of which 4 were waited for; matrix products, arithmetic and copies ran while one was open for 4% of the time, Pallas kernels for 11%

profile of v3, /device:TPU:1, one launch (start us, length us, event | category | flops | bytes accessed | tf_op | source)
XLA Modules:
  0.0 67.4 jit_solution(3236869575750040440)
XLA Ops:
  0.6 1.8 %side.1 = (bf16[4,12,8,256]{3,2,1,0:T(8,128)(2,1)}, bf16[4,12,8,256]{3,2,1,0:T(8,128)(2,1)}) custom-call(bf16[4,8,16,256]{3,2,1,0:T(8,128)(2,1)} %x.9, bf16[4,8,16,256]{3,2,1,0:T(8,128)(2,1)} %out_grad.5), custom_call_target="tpu_custom_call" | custom-call | bytes 1048576 | tf_op jit(solution)/shard_map/side/pallas_call | solution.py:373
  2.5 2.5 %collective-permute-start = (bf16[4,12,8,256]{3,2,1,0:T(8,128)(2,1)}, bf16[4,12,8,256]{3,2,1,0:T(8,128)(2,1)S(1)}, u32[]{:S(2)}, u32[]{:S(2)}) collective-permute-start(bf16[4,12,8,256]{3,2,1,0:T(8,128)(2,1)} %get-tuple-element.25), channel_id=1, source_target_pairs={{0,1},{1,2},{2,3},{3,4},{4,5},{5,6},{6,7},{7,8},{8,9},{9,10},{10,1... | collective-permute-start | bytes 589832 | tf_op jit(solution)/shard_map/ppermute | solution.py:404
  5.0 6.5 %collective-permute-start.1 = (bf16[4,12,8,256]{3,2,1,0:T(8,128)(2,1)}, bf16[4,12,8,256]{3,2,1,0:T(8,128)(2,1)S(1)}, u32[]{:S(2)}, u32[]{:S(2)}) collective-permute-start(bf16[4,12,8,256]{3,2,1,0:T(8,128)(2,1)} %get-tuple-element.26), channel_id=1, source_target_pairs={{1,0},{2,1},{3,2},{4,3},{5,4},{6,5},{7,6},{8,7},{9,8},{10,9},{11,1... | collective-permute-start | bytes 589832 | tf_op jit(solution)/shard_map/ppermute | solution.py:405
  11.5 1.0 %rev.3 = f32[8,9,3,9]{3,0,2,1:T(8,128)S(1)} reverse(f32[8,9,3,9]{3,0,2,1:T(8,128)} %param.9), dimensions={2,3} | reverse | bytes 15552 | tf_op jit(solution)/shard_map/rev | solution.py:466
  12.5 0.9 %copy.21 = f32[8,9,3,9]{3,2,1,0:T(4,128)S(1)} copy(f32[8,9,3,9]{3,0,2,1:T(8,128)} %param.9) | data formatting | bytes 15552
  13.6 0.1 reshape.31
  13.7 0.1 reshape.30
  13.9 0.1 concatenate.3.basis
  14.0 1.4 %table.1 = (bf16[5,9,48,128]{3,2,1,0:T(8,128)(2,1)S(1)}, bf16[4,9,32,128]{3,2,1,0:T(8,128)(2,1)S(1)}, bf16[256,512]{1,0:T(8,128)(2,1)S(1)}) custom-call(s32[32]{0:T(128)S(1)} %copy-done.3, s32[3,32]{1,0:T(4,128)S(1)} %bitcast.5, s32[1]{0:T(128)} %bitcast.2.first, f32[8,9,256]{2,1,0:T(8,128)S(1)} %concatenate.3.basis, bf16[4,8,16,256]{3,2,1,0:T(8,128)(2,1)S(1)} %copy-done), custom_call_target="tpu_custom_call" | custom-call | flops 16777216 | bytes 3145728 | tf_op jit(solution)/shard_map/table/pallas_call | solution.py:373
  15.5 0.7 %collective-permute-done.refs_2_.refs_4_.refs_8_.refs_10_.left = bf16[4,12,8,256]{3,2,1,0:T(8,128)(2,1)S(1)} collective-permute-done((bf16[4,12,8,256]{3,2,1,0:T(8,128)(2,1)}, bf16[4,12,8,256]{3,2,1,0:T(8,128)(2,1)S(1)}, u32[]{:S(2)}, u32[]{:S(2)}) %collective-permute-start) | collective-permute-done | bytes 196640 | tf_op jit(solution)/shard_map/ppermute | solution.py:404
  16.3 3.2 %collective-permute-start.3 = (bf16[4,11,8,256]{3,2,1,0:T(8,128)(2,1)S(1)}, bf16[4,11,8,256]{3,2,1,0:T(8,128)(2,1)S(1)}, u32[]{:S(2)}, u32[]{:S(2)}) collective-permute-start(bf16[4,11,8,256]{3,2,1,0:T(8,128)(2,1)S(1)} %get-tuple-element.28), channel_id=1, source_target_pairs={{32,0},{64,32},{96,64},{33,1},{65,33},{97,65},{34,2},{66,34},{98,6... | collective-permute-start | bytes 540680 | tf_op jit(solution)/shard_map/ppermute | solution.py:428
  19.5 3.0 %collective-permute-start.2 = (bf16[4,11,8,256]{3,2,1,0:T(8,128)(2,1)S(1)}, bf16[4,11,8,256]{3,2,1,0:T(8,128)(2,1)S(1)}, u32[]{:S(2)}, u32[]{:S(2)}) collective-permute-start(bf16[4,11,8,256]{3,2,1,0:T(8,128)(2,1)S(1)} %get-tuple-element.27.after), channel_id=1, source_target_pairs={{0,32},{32,64},{64,96},{1,33},{33,65},{65,97},{2,34},{34,66},{66,9... | collective-permute-start | bytes 540680 | tf_op jit(solution)/shard_map/ppermute | solution.py:427
  22.5 3.4 %inner.1 = (bf16[4,144,256]{2,1,0:T(8,128)(2,1)S(1)}, bf16[4,8,16,256]{3,2,1,0:T(8,128)(2,1)}) custom-call(bf16[4,8,16,256]{3,2,1,0:T(8,128)(2,1)S(1)} %copy-done, bf16[4,8,16,256]{3,2,1,0:T(8,128)(2,1)S(1)} %copy-done.1, bf16[5,9,48,128]{3,2,1,0:T(8,128)(2,1)S(1)} %get-tuple-element.23.near, ...), custom_call_target="tpu_custom_call" | custom-call | flops 3221225472 | bytes 4194304 | tf_op jit(solution)/shard_map/inner/pallas_call | solution.py:373
  25.9 4.3 %outer.1 = (bf16[256,1152]{1,0:T(8,128)(2,1)S(1)}, bf16[256,1152]{1,0:T(8,128)(2,1)S(1)}, bf16[4,272,256]{2,1,0:T(8,128)(2,1)}, bf16[4,8,16,256]{3,2,1,0:T(8,128)(2,1)}) custom-call(s32[1]{0:T(128)} %bitcast.core, bf16[4,8,16,256]{3,2,1,0:T(8,128)(2,1)S(1)} %copy-done, ...), custom_call_target="tpu_custom_call", output_to_operand_aliasing={{3}: (12, {})} | custom-call | flops 4294967296 | bytes 4194304 | tf_op jit(solution)/shard_map/outer/pallas_call | solution.py:373
  30.3 2.0 %collective-permute-done.4.got = bf16[256,1152]{1,0:T(8,128)(2,1)S(1)} collective-permute-done((bf16[256,1152]{1,0:T(8,128)(2,1)S(1)}, bf16[256,1152]{1,0:T(8,128)(2,1)S(1)}, u32[]{:S(2)}, u32[]{:S(2)}) %collective-permute-start.4) | collective-permute-done | bytes 589856 | tf_op jit(solution)/shard_map/ppermute | solution.py:437
  32.3 0.1 fold.1
  32.5 1.6 %collective-permute-start.6 = (bf16[64,1152]{1,0:T(8,128)(2,1)S(1)}, bf16[64,1152]{1,0:T(8,128)(2,1)S(1)}, u32[]{:S(2)}, u32[]{:S(2)}) collective-permute-start(bf16[64,1152]{1,0:T(8,128)(2,1)S(1)} %get-tuple-element.39), channel_id=1, source_target_pairs={{0,16},{1,17},{2,18},{3,19},{4,20},{5,21},{6,22},{7,23},{8,24},{9,... | collective-permute-start | bytes 442376 | tf_op jit(solution)/shard_map/ppermute | solution.py:445
  34.2 1.0 %collective-permute-start.7 = (bf16[64,1152]{1,0:T(8,128)(2,1)S(1)}, bf16[64,1152]{1,0:T(8,128)(2,1)S(1)}, u32[]{:S(2)}, u32[]{:S(2)}) collective-permute-start(bf16[64,1152]{1,0:T(8,128)(2,1)S(1)} %get-tuple-element.40), channel_id=1, source_target_pairs={{0,24},{1,25},{2,26},{3,27},{4,28},{5,29},{6,30},{7,31},{8,0},{9,1... | collective-permute-start | bytes 442376 | tf_op jit(solution)/shard_map/ppermute | solution.py:445
  35.2 2.9 %tail.1 = (bf16[4,8,16,256]{3,2,1,0:T(8,128)(2,1)}, f32[64,1152]{1,0:T(8,128)S(1)}) custom-call(bf16[4,272,256]{2,1,0:T(8,128)(2,1)S(1)} %copy-done.4, bf16[4,8,16,256]{3,2,1,0:T(8,128)(2,1)S(1)} %copy-done.1, bf16[4,9,32,128]{3,2,1,0:T(8,128)(2,1)S(1)} %get-tuple-element.24.refs_12_.far, ...), custom_call_target="tpu_custom_call", output_to_operand_aliasing={{1}: (4, {})} | custom-call | flops 2147483648 | bytes 4194304 | tf_op jit(solution)/shard_map/tail/pallas_call | solution.py:373
  38.1 4.1 %collective-permute-done.5.one = bf16[64,1152]{1,0:T(8,128)(2,1)S(1)} collective-permute-done((bf16[64,1152]{1,0:T(8,128)(2,1)S(1)}, bf16[64,1152]{1,0:T(8,128)(2,1)S(1)}, u32[]{:S(2)}, u32[]{:S(2)}) %collective-permute-start.5) | collective-permute-done | bytes 147488 | tf_op jit(solution)/shard_map/ppermute | solution.py:445
  42.2 0.3 collective-permute-done.7.three
  42.6 12.4 %all_to_all.10.shares = bf16[8,8,1152]{2,1,0:T(8,128)(2,1)S(1)} all-to-all(bf16[8,8,1152]{2,1,0:T(8,128)(2,1)S(1)} %join.1), channel_id=1, replica_groups={{0,1,2,3,4,5,6,7},{8,9,10,11,12,13,14,15},{16,17,18,19,20,21,22,23},{24..., dimensions={0} | all-to-all | bytes 294912 | tf_op jit(solution)/shard_map/all_to_all | solution.py:451
  55.0 11.7 %all_to_all.11.shares = bf16[8,8,1152]{2,1,0:T(8,128)(2,1)S(1)} all-to-all(bf16[8,8,1152]{2,1,0:T(8,128)(2,1)S(1)} %share.1), channel_id=1, replica_groups=mesh['ens'=2,'lat'=4,'lon'=32] {'ens','lat'}, dimensions={0} | all-to-all | bytes 294912 | tf_op jit(solution)/shard_map/all_to_all | solution.py:455
  66.8 0.7 place.1
  (24 shorter events, 0.5 us)
Async XLA Ops:
  2.5 13.7 %collective-permute-start = (bf16[4,12,8,256]{3,2,1,0:T(8,128)(2,1)}, bf16[4,12,8,256]{3,2,1,0:T(8,128)(2,1)S(1)}, u32[]{:S(2)}, u32[]{:S(2)}) collective-permute-start(bf16[4,12,8,256]{3,2,1,0:T(8,128)(2,1)} %get-tuple-element.25), channel_id=1, source_target_pairs={{0,1},{1,2},{2,3},{3,4},{4,5},{5,6},{6,7},{7,8},{8,9},{9,10},{10,1... | collective-permute-start | bytes 589832 | tf_op jit(solution)/shard_map/ppermute | solution.py:404
  5.0 11.2 %collective-permute-start.1 = (bf16[4,12,8,256]{3,2,1,0:T(8,128)(2,1)}, bf16[4,12,8,256]{3,2,1,0:T(8,128)(2,1)S(1)}, u32[]{:S(2)}, u32[]{:S(2)}) collective-permute-start(bf16[4,12,8,256]{3,2,1,0:T(8,128)(2,1)} %get-tuple-element.26), channel_id=1, source_target_pairs={{1,0},{2,1},{3,2},{4,3},{5,4},{6,5},{7,6},{8,7},{9,8},{10,9},{11,1... | collective-permute-start | bytes 589832 | tf_op jit(solution)/shard_map/ppermute | solution.py:405
  11.5 2.5 %copy-start = (bf16[4,8,16,256]{3,2,1,0:T(8,128)(2,1)S(1)}, bf16[4,8,16,256]{3,2,1,0:T(8,128)(2,1)}, u32[]{:S(2)}) copy-start(bf16[4,8,16,256]{3,2,1,0:T(8,128)(2,1)} %x.9) | copy-start | bytes 786436
  11.5 2.5 %copy-start.2 = (s32[32,3]{0,1:T(4,128)S(1)}, s32[32,3]{0,1:T(4,128)}, u32[]{:S(2)}) copy-start(s32[32,3]{0,1:T(4,128)} %param.11) | copy-start | bytes 1156
  11.5 2.5 %copy-start.3 = (s32[32]{0:T(128)S(1)}, s32[32]{0:T(128)}, u32[]{:S(2)}) copy-start(s32[32]{0:T(128)} %cycles.1) | copy-start | bytes 388
  13.5 2.8 %copy-start.1 = (bf16[4,8,16,256]{3,2,1,0:T(8,128)(2,1)S(1)}, bf16[4,8,16,256]{3,2,1,0:T(8,128)(2,1)}, u32[]{:S(2)}) copy-start(bf16[4,8,16,256]{3,2,1,0:T(8,128)(2,1)} %out_grad.5) | copy-start | bytes 786436
  16.3 9.6 %collective-permute-start.3 = (bf16[4,11,8,256]{3,2,1,0:T(8,128)(2,1)S(1)}, bf16[4,11,8,256]{3,2,1,0:T(8,128)(2,1)S(1)}, u32[]{:S(2)}, u32[]{:S(2)}) collective-permute-start(bf16[4,11,8,256]{3,2,1,0:T(8,128)(2,1)S(1)} %get-tuple-element.28), channel_id=1, source_target_pairs={{32,0},{64,32},{96,64},{33,1},{65,33},{97,65},{34,2},{66,34},{98,6... | collective-permute-start | bytes 540680 | tf_op jit(solution)/shard_map/ppermute | solution.py:428
  19.5 6.4 %collective-permute-start.2 = (bf16[4,11,8,256]{3,2,1,0:T(8,128)(2,1)S(1)}, bf16[4,11,8,256]{3,2,1,0:T(8,128)(2,1)S(1)}, u32[]{:S(2)}, u32[]{:S(2)}) collective-permute-start(bf16[4,11,8,256]{3,2,1,0:T(8,128)(2,1)S(1)} %get-tuple-element.27.after), channel_id=1, source_target_pairs={{0,32},{32,64},{64,96},{1,33},{33,65},{65,97},{2,34},{34,66},{66,9... | collective-permute-start | bytes 540680 | tf_op jit(solution)/shard_map/ppermute | solution.py:427
  30.2 5.0 %copy-start.4 = (bf16[4,272,256]{2,1,0:T(8,128)(2,1)S(1)}, bf16[4,272,256]{2,1,0:T(8,128)(2,1)}, u32[]{:S(2)}) copy-start(bf16[4,272,256]{2,1,0:T(8,128)(2,1)} %get-tuple-element.32.grads_in) | copy-start | bytes 1671172
  30.2 2.1 %collective-permute-start.4 = (bf16[256,1152]{1,0:T(8,128)(2,1)S(1)}, bf16[256,1152]{1,0:T(8,128)(2,1)S(1)}, u32[]{:S(2)}, u32[]{:S(2)}) collective-permute-start(bf16[256,1152]{1,0:T(8,128)(2,1)S(1)} %get-tuple-element.34), channel_id=1, source_target_pairs={{0,32},{32,0},{64,96},{96,64},{1,33},{33,1},{65,97},{97,65},{2,34}... | collective-permute-start | bytes 1769480 | tf_op jit(solution)/shard_map/ppermute | solution.py:437
  32.5 9.7 %collective-permute-start.5 = (bf16[64,1152]{1,0:T(8,128)(2,1)S(1)}, bf16[64,1152]{1,0:T(8,128)(2,1)S(1)}, u32[]{:S(2)}, u32[]{:S(2)}) collective-permute-start(bf16[64,1152]{1,0:T(8,128)(2,1)S(1)} %get-tuple-element.38), channel_id=1, source_target_pairs={{0,8},{1,9},{2,10},{3,11},{4,12},{5,13},{6,14},{7,15},{8,16},{9,17... | collective-permute-start | bytes 442376 | tf_op jit(solution)/shard_map/ppermute | solution.py:445
  32.5 9.6 %collective-permute-start.6 = (bf16[64,1152]{1,0:T(8,128)(2,1)S(1)}, bf16[64,1152]{1,0:T(8,128)(2,1)S(1)}, u32[]{:S(2)}, u32[]{:S(2)}) collective-permute-start(bf16[64,1152]{1,0:T(8,128)(2,1)S(1)} %get-tuple-element.39), channel_id=1, source_target_pairs={{0,16},{1,17},{2,18},{3,19},{4,20},{5,21},{6,22},{7,23},{8,24},{9,... | collective-permute-start | bytes 442376 | tf_op jit(solution)/shard_map/ppermute | solution.py:445
  34.2 8.3 %collective-permute-start.7 = (bf16[64,1152]{1,0:T(8,128)(2,1)S(1)}, bf16[64,1152]{1,0:T(8,128)(2,1)S(1)}, u32[]{:S(2)}, u32[]{:S(2)}) collective-permute-start(bf16[64,1152]{1,0:T(8,128)(2,1)S(1)} %get-tuple-element.40), channel_id=1, source_target_pairs={{0,24},{1,25},{2,26},{3,27},{4,28},{5,29},{6,30},{7,31},{8,0},{9,1... | collective-permute-start | bytes 442376 | tf_op jit(solution)/shard_map/ppermute | solution.py:445

commit v4 on v3

--- a/solution.py
+++ b/solution.py
@@ -35,14 +35,14 @@
     return [(i, i ^ 1) for i in range(4)]
 
 
-def y_shift(step):
-    return [(y * ZS + z, ((y + step) % YS) * ZS + z) for y in range(YS) for z in range(ZS)]
+def y_swap(step):
+    return [(y * ZS + z, (y ^ step) * ZS + z) for y in range(YS) for z in range(ZS)]
 
 
 def fold_kernel(y, mine, got, own, *sent):
     rows = C // YS
     for step in range(YS):
-        at = pl.multiple_of(lax.rem(y[0] + step, YS) * rows, rows)
+        at = pl.multiple_of((y[0] ^ step) * rows, rows)
         total = mine[pl.ds(at, rows), :].astype(F32) + got[pl.ds(at, rows), :].astype(F32)
         if step == 0:
             own[...] = total
@@ -394,10 +394,12 @@
         side_kernel,
         [FAR] * 2,
         [(shape, BF)] * 2,
-        (x, out_grad),
+        (
+            pltpu.with_memory_space_constraint(x, pltpu.HBM),
+            pltpu.with_memory_space_constraint(out_grad, pltpu.HBM),
+        ),
         "side",
         scratch=[(x.shape, BF)] * 2,
-        mib=60,
         sems=2,
     )
     count = lax.axis_size("lon")
@@ -442,7 +444,7 @@
         (y_index, mine, got),
         "fold",
     )
-    parts = [lax.ppermute(sent[step - 1], "lon", y_shift(step)) for step in range(1, YS)]
+    parts = [lax.ppermute(sent[step - 1], "lon", y_swap(step)) for step in (2, 1, 3)]
     extra, own = behind(own)
     (joined,) = call(
         join_kernel, [VM] * 4, [((ZS, share_rows, half), BF)], (own, *parts), "join"

time: 67.7 us -> 66.2 us (0.978)
  blocking collectives: 24.1 us -> 23.1 us
  Pallas kernels: 14.8 us -> 14.1 us
    all_to_all x1, blocking collectives: 12.4 us -> 11.4 us  [reduce_gradient(): lax.all_to_all(joined, 'lon', 0, 0, axis_index_groups=groups, tiled=True)]
    pallas_call x9, Pallas kernels: 14.7 us -> 14 us  [call(): pl.pallas_call(kernel, out_shape=outs, in_specs=ins, out_specs=out_specs,...]
  transfers between devices with their start and end apart: 8 -> 8, of which waited for: 4 -> 5; matrix products, arithmetic and copies ran while one was open for 4% -> 4% of each run, Pallas kernels for 11% -> 12%
where the time goes in v4:
time: 66.2 us; the launch traced here: 65.9 us
  blocking collectives  23.1 us (35%)
  starting transfers between devices  18.6 us (28%)
  Pallas kernels  14.1 us (21%)
  waiting for transfers between devices  6.8 us (10%)
  local copies, waits for them, and re-layouts  2.46 us (4%)
  between operations  0.85 us (1%)
    pallas_call x9, Pallas kernels, call(): pl.pallas_call(kernel, out_shape=outs, in_specs=ins, out_specs=out_specs,...  14 us
    all_to_all x1, blocking collectives, reduce_gradient(): shares = lax.all_to_all(share, ('ens', 'lat'), 0, 0, tiled=True)  11.7 us
    all_to_all x1, blocking collectives, reduce_gradient(): lax.all_to_all(joined, 'lon', 0, 0, axis_index_groups=groups, tiled=True)  11.4 us
    ppermute x1, starting transfers between devices, send_sides(): lax.ppermute(to_left, 'lon', [((i + 1) % count, i) for i in range(count)])  6.48 us
    ppermute x3, waiting for transfers between devices, reduce_gradient(): lax.ppermute(sent[step - 1], 'lon', y_swap(step))  4.3 us
    ppermute x3, starting transfers between devices, reduce_gradient(): lax.ppermute(sent[step - 1], 'lon', y_swap(step))  3.34 us
    ppermute x1, starting transfers between devices, send_rims(): bottom = lax.ppermute(down, 'lat', [(i + 1, i) for i in range(count - 1)])  3.16 us
    ppermute x1, starting transfers between devices, send_rims(): top = lax.ppermute(up, 'lat', [(i, i + 1) for i in range(count - 1)])  3.02 us
  transfers between devices with their start and end apart: 8, of which 5 were waited for; matrix products, arithmetic and copies ran while one was open for 4% of the time, Pallas kernels for 12%

profile of v4, /device:TPU:1, one launch (start us, length us, event | category | flops | bytes accessed | tf_op | source)
XLA Modules:
  0.0 65.9 jit_solution(5749481434213233557)
XLA Ops:
  0.6 1.1 %side.1 = (bf16[4,12,8,256]{3,2,1,0:T(8,128)(2,1)S(1)}, bf16[4,12,8,256]{3,2,1,0:T(8,128)(2,1)S(1)}) custom-call(bf16[4,8,16,256]{3,2,1,0:T(8,128)(2,1)} %x.9, bf16[4,8,16,256]{3,2,1,0:T(8,128)(2,1)} %out_grad.5), custom_call_target="tpu_custom_call" | custom-call | bytes 1048576 | tf_op jit(solution)/shard_map/side/pallas_call | solution.py:373
  1.7 2.5 %collective-permute-start = (bf16[4,12,8,256]{3,2,1,0:T(8,128)(2,1)S(1)}, bf16[4,12,8,256]{3,2,1,0:T(8,128)(2,1)S(1)}, u32[]{:S(2)}, u32[]{:S(2)}) collective-permute-start(bf16[4,12,8,256]{3,2,1,0:T(8,128)(2,1)S(1)} %get-tuple-element.25), channel_id=1, source_target_pairs={{0,1},{1,2},{2,3},{3,4},{4,5},{5,6},{6,7},{7,8},{8,9},{9,10},{10,1... | collective-permute-start | bytes 589832 | tf_op jit(solution)/shard_map/ppermute | solution.py:406
  4.3 6.5 %collective-permute-start.1 = (bf16[4,12,8,256]{3,2,1,0:T(8,128)(2,1)S(1)}, bf16[4,12,8,256]{3,2,1,0:T(8,128)(2,1)S(1)}, u32[]{:S(2)}, u32[]{:S(2)}) collective-permute-start(bf16[4,12,8,256]{3,2,1,0:T(8,128)(2,1)S(1)} %get-tuple-element.26), channel_id=1, source_target_pairs={{1,0},{2,1},{3,2},{4,3},{5,4},{6,5},{7,6},{8,7},{9,8},{10,9},{11,1... | collective-permute-start | bytes 589832 | tf_op jit(solution)/shard_map/ppermute | solution.py:407
  10.8 1.0 %rev.3 = f32[8,9,3,9]{3,0,2,1:T(8,128)S(1)} reverse(f32[8,9,3,9]{3,0,2,1:T(8,128)} %param.9), dimensions={2,3} | reverse | bytes 15552 | tf_op jit(solution)/shard_map/rev | solution.py:468
  11.8 0.9 %copy.21 = f32[8,9,3,9]{3,2,1,0:T(4,128)S(1)} copy(f32[8,9,3,9]{3,0,2,1:T(8,128)} %param.9) | data formatting | bytes 15552
  13.1 0.1 concatenate.3.basis
  13.3 1.4 %table.1 = (bf16[5,9,48,128]{3,2,1,0:T(8,128)(2,1)S(1)}, bf16[4,9,32,128]{3,2,1,0:T(8,128)(2,1)S(1)}, bf16[256,512]{1,0:T(8,128)(2,1)S(1)}) custom-call(s32[32]{0:T(128)S(1)} %copy-done.3, s32[3,32]{1,0:T(4,128)S(1)} %bitcast.5, s32[1]{0:T(128)} %bitcast.2.first, f32[8,9,256]{2,1,0:T(8,128)S(1)} %concatenate.3.basis, bf16[4,8,16,256]{3,2,1,0:T(8,128)(2,1)S(1)} %copy-done), custom_call_target="tpu_custom_call" | custom-call | flops 16777216 | bytes 3145728 | tf_op jit(solution)/shard_map/table/pallas_call | solution.py:373
  14.7 0.5 collective-permute-done.refs_2_.refs_4_.refs_8_.refs_10_.left
  15.4 3.2 %collective-permute-start.3 = (bf16[4,11,8,256]{3,2,1,0:T(8,128)(2,1)S(1)}, bf16[4,11,8,256]{3,2,1,0:T(8,128)(2,1)S(1)}, u32[]{:S(2)}, u32[]{:S(2)}) collective-permute-start(bf16[4,11,8,256]{3,2,1,0:T(8,128)(2,1)S(1)} %get-tuple-element.28), channel_id=1, source_target_pairs={{32,0},{64,32},{96,64},{33,1},{65,33},{97,65},{34,2},{66,34},{98,6... | collective-permute-start | bytes 540680 | tf_op jit(solution)/shard_map/ppermute | solution.py:430
  18.5 3.0 %collective-permute-start.2 = (bf16[4,11,8,256]{3,2,1,0:T(8,128)(2,1)S(1)}, bf16[4,11,8,256]{3,2,1,0:T(8,128)(2,1)S(1)}, u32[]{:S(2)}, u32[]{:S(2)}) collective-permute-start(bf16[4,11,8,256]{3,2,1,0:T(8,128)(2,1)S(1)} %get-tuple-element.27.after), channel_id=1, source_target_pairs={{0,32},{32,64},{64,96},{1,33},{33,65},{65,97},{2,34},{34,66},{66,9... | collective-permute-start | bytes 540680 | tf_op jit(solution)/shard_map/ppermute | solution.py:429
  21.6 3.4 %inner.1 = (bf16[4,144,256]{2,1,0:T(8,128)(2,1)S(1)}, bf16[4,8,16,256]{3,2,1,0:T(8,128)(2,1)}) custom-call(bf16[4,8,16,256]{3,2,1,0:T(8,128)(2,1)S(1)} %copy-done, bf16[4,8,16,256]{3,2,1,0:T(8,128)(2,1)S(1)} %copy-done.1, bf16[5,9,48,128]{3,2,1,0:T(8,128)(2,1)S(1)} %get-tuple-element.23.near, ...), custom_call_target="tpu_custom_call" | custom-call | flops 3221225472 | bytes 4194304 | tf_op jit(solution)/shard_map/inner/pallas_call | solution.py:373
  25.0 4.3 %outer.1 = (bf16[256,1152]{1,0:T(8,128)(2,1)S(1)}, bf16[256,1152]{1,0:T(8,128)(2,1)S(1)}, bf16[4,272,256]{2,1,0:T(8,128)(2,1)}, bf16[4,8,16,256]{3,2,1,0:T(8,128)(2,1)}) custom-call(s32[1]{0:T(128)} %bitcast.core, bf16[4,8,16,256]{3,2,1,0:T(8,128)(2,1)S(1)} %copy-done, ...), custom_call_target="tpu_custom_call", output_to_operand_aliasing={{3}: (12, {})} | custom-call | flops 4294967296 | bytes 4194304 | tf_op jit(solution)/shard_map/outer/pallas_call | solution.py:373
  29.4 2.0 %collective-permute-done.4.got = bf16[256,1152]{1,0:T(8,128)(2,1)S(1)} collective-permute-done((bf16[256,1152]{1,0:T(8,128)(2,1)S(1)}, bf16[256,1152]{1,0:T(8,128)(2,1)S(1)}, u32[]{:S(2)}, u32[]{:S(2)}) %collective-permute-start.4) | collective-permute-done | bytes 589856 | tf_op jit(solution)/shard_map/ppermute | solution.py:439
  31.4 0.1 fold.1
  31.5 0.4 collective-permute-start.5
  31.9 0.7 %collective-permute-start.6 = (bf16[64,1152]{1,0:T(8,128)(2,1)S(1)}, bf16[64,1152]{1,0:T(8,128)(2,1)S(1)}, u32[]{:S(2)}, u32[]{:S(2)}) collective-permute-start(bf16[64,1152]{1,0:T(8,128)(2,1)S(1)} %get-tuple-element.39), channel_id=1, source_target_pairs={{0,8},{1,9},{2,10},{3,11},{4,12},{5,13},{6,14},{7,15},{8,0},{9,1},... | collective-permute-start | bytes 442376 | tf_op jit(solution)/shard_map/ppermute | solution.py:447
  32.6 2.2 %collective-permute-start.7 = (bf16[64,1152]{1,0:T(8,128)(2,1)S(1)}, bf16[64,1152]{1,0:T(8,128)(2,1)S(1)}, u32[]{:S(2)}, u32[]{:S(2)}) collective-permute-start(bf16[64,1152]{1,0:T(8,128)(2,1)S(1)} %get-tuple-element.40), channel_id=1, source_target_pairs={{0,24},{1,25},{2,26},{3,27},{4,28},{5,29},{6,30},{7,31},{8,16},{9,... | collective-permute-start | bytes 442376 | tf_op jit(solution)/shard_map/ppermute | solution.py:447
  34.9 2.9 %tail.1 = (bf16[4,8,16,256]{3,2,1,0:T(8,128)(2,1)}, f32[64,1152]{1,0:T(8,128)S(1)}) custom-call(bf16[4,272,256]{2,1,0:T(8,128)(2,1)S(1)} %copy-done.4, bf16[4,8,16,256]{3,2,1,0:T(8,128)(2,1)S(1)} %copy-done.1, bf16[4,9,32,128]{3,2,1,0:T(8,128)(2,1)S(1)} %get-tuple-element.24.refs_12_.far, ...), custom_call_target="tpu_custom_call", output_to_operand_aliasing={{1}: (4, {})} | custom-call | flops 2147483648 | bytes 4194304 | tf_op jit(solution)/shard_map/tail/pallas_call | solution.py:373
  37.7 0.7 %collective-permute-done.5.one = bf16[64,1152]{1,0:T(8,128)(2,1)S(1)} collective-permute-done((bf16[64,1152]{1,0:T(8,128)(2,1)S(1)}, bf16[64,1152]{1,0:T(8,128)(2,1)S(1)}, u32[]{:S(2)}, u32[]{:S(2)}) %collective-permute-start.5) | collective-permute-done | bytes 147488 | tf_op jit(solution)/shard_map/ppermute | solution.py:447
  38.4 1.2 %collective-permute-done.6.two = bf16[64,1152]{1,0:T(8,128)(2,1)S(1)} collective-permute-done((bf16[64,1152]{1,0:T(8,128)(2,1)S(1)}, bf16[64,1152]{1,0:T(8,128)(2,1)S(1)}, u32[]{:S(2)}, u32[]{:S(2)}) %collective-permute-start.6) | collective-permute-done | bytes 147488 | tf_op jit(solution)/shard_map/ppermute | solution.py:447
  39.6 2.4 %collective-permute-done.7.three = bf16[64,1152]{1,0:T(8,128)(2,1)S(1)} collective-permute-done((bf16[64,1152]{1,0:T(8,128)(2,1)S(1)}, bf16[64,1152]{1,0:T(8,128)(2,1)S(1)}, u32[]{:S(2)}, u32[]{:S(2)}) %collective-permute-start.7) | collective-permute-done | bytes 147488 | tf_op jit(solution)/shard_map/ppermute | solution.py:447
  42.1 11.4 %all_to_all.10.shares = bf16[8,8,1152]{2,1,0:T(8,128)(2,1)S(1)} all-to-all(bf16[8,8,1152]{2,1,0:T(8,128)(2,1)S(1)} %join.1), channel_id=1, replica_groups={{0,1,2,3,4,5,6,7},{8,9,10,11,12,13,14,15},{16,17,18,19,20,21,22,23},{24..., dimensions={0} | all-to-all | bytes 294912 | tf_op jit(solution)/shard_map/all_to_all | solution.py:453
  53.5 11.7 %all_to_all.11.shares = bf16[8,8,1152]{2,1,0:T(8,128)(2,1)S(1)} all-to-all(bf16[8,8,1152]{2,1,0:T(8,128)(2,1)S(1)} %share.1), channel_id=1, replica_groups=mesh['ens'=2,'lat'=4,'lon'=32] {'ens','lat'}, dimensions={0} | all-to-all | bytes 294912 | tf_op jit(solution)/shard_map/all_to_all | solution.py:457
  65.3 0.7 place.1
  (24 shorter events, 0.7 us)
Async XLA Ops:
  1.7 13.5 %collective-permute-start = (bf16[4,12,8,256]{3,2,1,0:T(8,128)(2,1)S(1)}, bf16[4,12,8,256]{3,2,1,0:T(8,128)(2,1)S(1)}, u32[]{:S(2)}, u32[]{:S(2)}) collective-permute-start(bf16[4,12,8,256]{3,2,1,0:T(8,128)(2,1)S(1)} %get-tuple-element.25), channel_id=1, source_target_pairs={{0,1},{1,2},{2,3},{3,4},{4,5},{5,6},{6,7},{7,8},{8,9},{9,10},{10,1... | collective-permute-start | bytes 589832 | tf_op jit(solution)/shard_map/ppermute | solution.py:406
  4.3 11.0 %collective-permute-start.1 = (bf16[4,12,8,256]{3,2,1,0:T(8,128)(2,1)S(1)}, bf16[4,12,8,256]{3,2,1,0:T(8,128)(2,1)S(1)}, u32[]{:S(2)}, u32[]{:S(2)}) collective-permute-start(bf16[4,12,8,256]{3,2,1,0:T(8,128)(2,1)S(1)} %get-tuple-element.26), channel_id=1, source_target_pairs={{1,0},{2,1},{3,2},{4,3},{5,4},{6,5},{7,6},{8,7},{9,8},{10,9},{11,1... | collective-permute-start | bytes 589832 | tf_op jit(solution)/shard_map/ppermute | solution.py:407
  10.7 2.5 %copy-start = (bf16[4,8,16,256]{3,2,1,0:T(8,128)(2,1)S(1)}, bf16[4,8,16,256]{3,2,1,0:T(8,128)(2,1)}, u32[]{:S(2)}) copy-start(bf16[4,8,16,256]{3,2,1,0:T(8,128)(2,1)} %x.9) | copy-start | bytes 786436
  10.8 2.5 %copy-start.2 = (s32[32,3]{0,1:T(4,128)S(1)}, s32[32,3]{0,1:T(4,128)}, u32[]{:S(2)}) copy-start(s32[32,3]{0,1:T(4,128)} %param.11) | copy-start | bytes 1156
  10.8 2.5 %copy-start.3 = (s32[32]{0:T(128)S(1)}, s32[32]{0:T(128)}, u32[]{:S(2)}) copy-start(s32[32]{0:T(128)} %cycles.1) | copy-start | bytes 388
  12.7 2.5 %copy-start.1 = (bf16[4,8,16,256]{3,2,1,0:T(8,128)(2,1)S(1)}, bf16[4,8,16,256]{3,2,1,0:T(8,128)(2,1)}, u32[]{:S(2)}) copy-start(bf16[4,8,16,256]{3,2,1,0:T(8,128)(2,1)} %out_grad.5) | copy-start | bytes 786436
  15.4 9.6 %collective-permute-start.3 = (bf16[4,11,8,256]{3,2,1,0:T(8,128)(2,1)S(1)}, bf16[4,11,8,256]{3,2,1,0:T(8,128)(2,1)S(1)}, u32[]{:S(2)}, u32[]{:S(2)}) collective-permute-start(bf16[4,11,8,256]{3,2,1,0:T(8,128)(2,1)S(1)} %get-tuple-element.28), channel_id=1, source_target_pairs={{32,0},{64,32},{96,64},{33,1},{65,33},{97,65},{34,2},{66,34},{98,6... | collective-permute-start | bytes 540680 | tf_op jit(solution)/shard_map/ppermute | solution.py:430
  18.5 6.4 %collective-permute-start.2 = (bf16[4,11,8,256]{3,2,1,0:T(8,128)(2,1)S(1)}, bf16[4,11,8,256]{3,2,1,0:T(8,128)(2,1)S(1)}, u32[]{:S(2)}, u32[]{:S(2)}) collective-permute-start(bf16[4,11,8,256]{3,2,1,0:T(8,128)(2,1)S(1)} %get-tuple-element.27.after), channel_id=1, source_target_pairs={{0,32},{32,64},{64,96},{1,33},{33,65},{65,97},{2,34},{34,66},{66,9... | collective-permute-start | bytes 540680 | tf_op jit(solution)/shard_map/ppermute | solution.py:429
  29.3 5.6 %copy-start.4 = (bf16[4,272,256]{2,1,0:T(8,128)(2,1)S(1)}, bf16[4,272,256]{2,1,0:T(8,128)(2,1)}, u32[]{:S(2)}) copy-start(bf16[4,272,256]{2,1,0:T(8,128)(2,1)} %get-tuple-element.32.grads_in) | copy-start | bytes 1671172
  29.3 2.1 %collective-permute-start.4 = (bf16[256,1152]{1,0:T(8,128)(2,1)S(1)}, bf16[256,1152]{1,0:T(8,128)(2,1)S(1)}, u32[]{:S(2)}, u32[]{:S(2)}) collective-permute-start(bf16[256,1152]{1,0:T(8,128)(2,1)S(1)} %get-tuple-element.34), channel_id=1, source_target_pairs={{0,32},{32,0},{64,96},{96,64},{1,33},{33,1},{65,97},{97,65},{2,34}... | collective-permute-start | bytes 1769480 | tf_op jit(solution)/shard_map/ppermute | solution.py:439
  31.5 6.9 %collective-permute-start.5 = (bf16[64,1152]{1,0:T(8,128)(2,1)S(1)}, bf16[64,1152]{1,0:T(8,128)(2,1)S(1)}, u32[]{:S(2)}, u32[]{:S(2)}) collective-permute-start(bf16[64,1152]{1,0:T(8,128)(2,1)S(1)} %get-tuple-element.38), channel_id=1, source_target_pairs={{0,16},{1,17},{2,18},{3,19},{4,20},{5,21},{6,22},{7,23},{8,24},{9,... | collective-permute-start | bytes 442376 | tf_op jit(solution)/shard_map/ppermute | solution.py:447
  31.9 7.7 %collective-permute-start.6 = (bf16[64,1152]{1,0:T(8,128)(2,1)S(1)}, bf16[64,1152]{1,0:T(8,128)(2,1)S(1)}, u32[]{:S(2)}, u32[]{:S(2)}) collective-permute-start(bf16[64,1152]{1,0:T(8,128)(2,1)S(1)} %get-tuple-element.39), channel_id=1, source_target_pairs={{0,8},{1,9},{2,10},{3,11},{4,12},{5,13},{6,14},{7,15},{8,0},{9,1},... | collective-permute-start | bytes 442376 | tf_op jit(solution)/shard_map/ppermute | solution.py:447
  32.6 9.4 %collective-permute-start.7 = (bf16[64,1152]{1,0:T(8,128)(2,1)S(1)}, bf16[64,1152]{1,0:T(8,128)(2,1)S(1)}, u32[]{:S(2)}, u32[]{:S(2)}) collective-permute-start(bf16[64,1152]{1,0:T(8,128)(2,1)S(1)} %get-tuple-element.40), channel_id=1, source_target_pairs={{0,24},{1,25},{2,26},{3,27},{4,28},{5,29},{6,30},{7,31},{8,16},{9,... | collective-permute-start | bytes 442376 | tf_op jit(solution)/shard_map/ppermute | solution.py:447

commit v5 on v4

--- a/solution.py
+++ b/solution.py
@@ -166,8 +166,18 @@
 
 
 def rim_kernel(*refs):
-    rim_rows(*refs[0:6], 4, refs[13])
-    rim_rows(*refs[6:12], 0, refs[14])
+    even = refs[13][0] == 0
+    pair, cross = refs[14], refs[15]
+
+    @pl.when(even)
+    def _():
+        rim_rows(*refs[0:6], 4, pair)
+        rim_rows(*refs[6:12], 0, cross)
+
+    @pl.when(jnp.logical_not(even))
+    def _():
+        rim_rows(*refs[6:12], 0, pair)
+        rim_rows(*refs[0:6], 4, cross)
 
 
 def adjoint_rows(far, grads, back):
@@ -261,7 +271,7 @@
 
 
 def outer_kernel(
-    scale, core, x, x_turned, out_grad, near, far, top, bottom, left, right, middle, weight_in,
+    scale, core, x, x_turned, out_grad, near, far, paired, crossed, left, right, middle, weight_in,
     tie, mine, other, grads_out, result_out,
     wide, cotangent, features, mixed, result, grads, back, weight, sems,
 ):
@@ -269,7 +279,7 @@
     copy.start()
     last = G_ROWS // 2 - 1
 
-    def gather(m, carry):
+    def gather(top, bottom, m, carry):
         for r in range(2):
             for at, rim in ((r, top), (6 + r, bottom)):
                 row = jnp.concatenate([rim[m, 4 * r + t].astype(F32) for t in range(4)], axis=0)
@@ -289,7 +299,16 @@
             spread_pair(near[p], wide[m, 128 * q : 128 * q + 128], features, start)
         return carry
 
-    lax.fori_loop(0, M, gather, 0)
+    first = core[0] == 0
+
+    @pl.when(first)
+    def _():
+        lax.fori_loop(0, M, functools.partial(gather, crossed, paired), 0)
+
+    @pl.when(jnp.logical_not(first))
+    def _():
+        lax.fori_loop(0, M, functools.partial(gather, paired, crossed), 0)
+
     copy.wait()
     mixed[...] = jnp.dot(features[...], weight[...], preferred_element_type=F32).reshape(
         mixed.shape
@@ -316,7 +335,6 @@
     for copy in copies:
         copy.start()
     adjoint_rows(far, grads, back)
-    first = core[0] == 0
     for k in range(K):
         part = scale * jnp.dot(
             x_turned[...], back[:, k * C : (k + 1) * C], preferred_element_type=F32
@@ -408,27 +426,26 @@
     return left, right
 
 
-def send_rims(x, out_grad, left, right, after):
+def send_rims(core, x, out_grad, left, right, after):
     shape = (M, 11, 8, C)
     whole = pl.BlockSpec(shape, lambda i: (0, 0, 0, 0))
     ins = []
     for x_at, g_at in ((ROWS // 2 - 1, ROWS - 1), (0, 0)):
         ins += [edge(2, x_at, COLS), edge(1, g_at, COLS)]
         ins += [edge(2, x_at, 8)] * 2 + [edge(1, ROWS + g_at // 2, 8)] * 2
-    up, down = pl.pallas_call(
+    pair, cross = pl.pallas_call(
         rim_kernel,
         grid=(1,),
         out_shape=[jax.ShapeDtypeStruct(shape, BF)] * 2,
-        in_specs=ins + [KEPT],
+        in_specs=ins + [KEPT, SM],
         out_specs=[whole] * 2,
         cost_estimate=pl.CostEstimate(flops=0, bytes_accessed=1 << 18, transcendentals=0),
         compiler_params=pltpu.CompilerParams(vmem_limit_bytes=6 << 20),
         name="rim",
-    )(*((x, out_grad, left, right, left, right) * 2), after)
-    count = lax.axis_size("lat")
-    top = lax.ppermute(up, "lat", [(i, i + 1) for i in range(count - 1)])
-    bottom = lax.ppermute(down, "lat", [(i + 1, i) for i in range(count - 1)])
-    return up, top, bottom
+    )(*((x, out_grad, left, right, left, right) * 2), after, core)
+    crossed = lax.ppermute(cross, "lat", [(1, 2), (2, 1)])
+    paired = lax.ppermute(pair, "lat", core_swap())
+    return pair, paired, crossed
 
 
 def reduce_gradient(mine, other, behind):
@@ -483,7 +500,8 @@
         flops=1 << 24,
         moved=3 << 20,
     )
-    up, top, bottom = send_rims(members_in, out_grad, left, right, far)
+    core = lax.rem(lat, CORES).reshape(1)
+    pair, paired, crossed = send_rims(core, members_in, out_grad, left, right, far)
     flat_weight = pltpu.with_memory_space_constraint(weight.reshape(K * C, C), pltpu.HBM)
     cell_count = (
         M * lax.axis_size("ens") * ROWS * lax.axis_size("lat") * COLS * lax.axis_size("lon")
@@ -494,7 +512,7 @@
         inner_kernel,
         [VM] * 5 + [FAR, KEPT],
         [((M, inner, C), BF)],
-        (members_in, out_grad, near, left, right, flat_weight, up),
+        (members_in, out_grad, near, left, right, flat_weight, pair),
         "inner",
         scratch=[
             ((M, ROWS * WIDE, C), BF),
@@ -516,14 +534,14 @@
         [SM] + [VM] * 10 + [FAR],
         [(half_shape, BF)] * 2,
         (
-            lax.rem(lat, CORES).reshape(1),
+            core,
             members_in,
             x_turned,
             out_grad,
             near,
             far,
-            top,
-            bottom,
+            paired,
+            crossed,
             left,
             right,
             middle,

time: 66.2 us -> 64.5 us (0.974)
  starting transfers between devices: 18.6 us -> 17.3 us
    ppermute x2, starting transfers between devices: 6.18 us -> 4.35 us  [the longest x1 4.26 us: send_rims(): crossed = lax.ppermute(cross, 'lat', [(1, 2), (2, 1)])]
where the time goes in v5:
time: 64.5 us; the launch traced here: 64.2 us
  blocking collectives  23.1 us (36%)
  starting transfers between devices  17.3 us (27%)
  Pallas kernels  14.1 us (22%)
  waiting for transfers between devices  6.45 us (10%)
  local copies, waits for them, and re-layouts  2.46 us (4%)
  between operations  0.83 us (1%)
    pallas_call x9, Pallas kernels, call(): pl.pallas_call(kernel, out_shape=outs, in_specs=ins, out_specs=out_specs,...  14 us
    all_to_all x1, blocking collectives, reduce_gradient(): shares = lax.all_to_all(share, ('ens', 'lat'), 0, 0, tiled=True)  11.8 us
    all_to_all x1, blocking collectives, reduce_gradient(): lax.all_to_all(joined, 'lon', 0, 0, axis_index_groups=groups, tiled=True)  11.3 us
    ppermute x1, starting transfers between devices, send_sides(): lax.ppermute(to_left, 'lon', [((i + 1) % count, i) for i in range(count)])  6.48 us
    ppermute x3, waiting for transfers between devices, reduce_gradient(): lax.ppermute(sent[step - 1], 'lon', y_swap(step))  4.3 us
    ppermute x1, starting transfers between devices, send_rims(): crossed = lax.ppermute(cross, 'lat', [(1, 2), (2, 1)])  4.26 us
    ppermute x3, starting transfers between devices, reduce_gradient(): lax.ppermute(sent[step - 1], 'lon', y_swap(step))  3.34 us
    ppermute x1, starting transfers between devices, send_sides(): lax.ppermute(to_right, 'lon', [(i, (i + 1) % count) for i in range(count)])  2.53 us
  transfers between devices with their start and end apart: 8, of which 5 were waited for; matrix products, arithmetic and copies ran while one was open for 4% of the time, Pallas kernels for 12%

profile of v5, /device:TPU:1, one launch (start us, length us, event | category | flops | bytes accessed | tf_op | source)
XLA Modules:
  0.0 64.2 jit_solution(4857274283247342208)
XLA Ops:
  0.6 1.1 %side.1 = (bf16[4,12,8,256]{3,2,1,0:T(8,128)(2,1)S(1)}, bf16[4,12,8,256]{3,2,1,0:T(8,128)(2,1)S(1)}) custom-call(bf16[4,8,16,256]{3,2,1,0:T(8,128)(2,1)} %x.9, bf16[4,8,16,256]{3,2,1,0:T(8,128)(2,1)} %out_grad.5), custom_call_target="tpu_custom_call" | custom-call | bytes 1048576 | tf_op jit(solution)/shard_map/side/pallas_call | solution.py:391
  1.7 2.5 %collective-permute-start = (bf16[4,12,8,256]{3,2,1,0:T(8,128)(2,1)S(1)}, bf16[4,12,8,256]{3,2,1,0:T(8,128)(2,1)S(1)}, u32[]{:S(2)}, u32[]{:S(2)}) collective-permute-start(bf16[4,12,8,256]{3,2,1,0:T(8,128)(2,1)S(1)} %get-tuple-element.25), channel_id=1, source_target_pairs={{0,1},{1,2},{2,3},{3,4},{4,5},{5,6},{6,7},{7,8},{8,9},{9,10},{10,1... | collective-permute-start | bytes 589832 | tf_op jit(solution)/shard_map/ppermute | solution.py:424
  4.3 6.5 %collective-permute-start.1 = (bf16[4,12,8,256]{3,2,1,0:T(8,128)(2,1)S(1)}, bf16[4,12,8,256]{3,2,1,0:T(8,128)(2,1)S(1)}, u32[]{:S(2)}, u32[]{:S(2)}) collective-permute-start(bf16[4,12,8,256]{3,2,1,0:T(8,128)(2,1)S(1)} %get-tuple-element.26), channel_id=1, source_target_pairs={{1,0},{2,1},{3,2},{4,3},{5,4},{6,5},{7,6},{8,7},{9,8},{10,9},{11,1... | collective-permute-start | bytes 589832 | tf_op jit(solution)/shard_map/ppermute | solution.py:425
  10.8 1.0 %rev.3 = f32[8,9,3,9]{3,0,2,1:T(8,128)S(1)} reverse(f32[8,9,3,9]{3,0,2,1:T(8,128)} %param.9), dimensions={2,3} | reverse | bytes 15552 | tf_op jit(solution)/shard_map/rev | solution.py:485
  11.8 0.9 %copy.21 = f32[8,9,3,9]{3,2,1,0:T(4,128)S(1)} copy(f32[8,9,3,9]{3,0,2,1:T(8,128)} %param.9) | data formatting | bytes 15552
  13.1 0.1 concatenate.3.basis
  13.3 1.4 %table.1 = (bf16[5,9,48,128]{3,2,1,0:T(8,128)(2,1)S(1)}, bf16[4,9,32,128]{3,2,1,0:T(8,128)(2,1)S(1)}, bf16[256,512]{1,0:T(8,128)(2,1)S(1)}) custom-call(s32[32]{0:T(128)S(1)} %copy-done.3, s32[3,32]{1,0:T(4,128)S(1)} %bitcast.5, s32[1]{0:T(128)} %bitcast.2.first, f32[8,9,256]{2,1,0:T(8,128)S(1)} %concatenate.3.basis, bf16[4,8,16,256]{3,2,1,0:T(8,128)(2,1)S(1)} %copy-done), custom_call_target="tpu_custom_call" | custom-call | flops 16777216 | bytes 3145728 | tf_op jit(solution)/shard_map/table/pallas_call | solution.py:391
  14.7 0.5 collective-permute-done.refs_2_.refs_4_.refs_8_.refs_10_.left
  15.4 4.3 %collective-permute-start.3 = (bf16[4,11,8,256]{3,2,1,0:T(8,128)(2,1)S(1)}, bf16[4,11,8,256]{3,2,1,0:T(8,128)(2,1)S(1)}, u32[]{:S(2)}, u32[]{:S(2)}) collective-permute-start(bf16[4,11,8,256]{3,2,1,0:T(8,128)(2,1)S(1)} %get-tuple-element.28), channel_id=1, source_target_pairs={{32,64},{64,32},{33,65},{65,33},{34,66},{66,34},{35,67},{67,35},{3... | collective-permute-start | bytes 540680 | tf_op jit(solution)/shard_map/ppermute | solution.py:446
  19.7 3.4 %inner.1 = (bf16[4,144,256]{2,1,0:T(8,128)(2,1)S(1)}, bf16[4,8,16,256]{3,2,1,0:T(8,128)(2,1)}) custom-call(bf16[4,8,16,256]{3,2,1,0:T(8,128)(2,1)S(1)} %copy-done, bf16[4,8,16,256]{3,2,1,0:T(8,128)(2,1)S(1)} %copy-done.1, bf16[5,9,48,128]{3,2,1,0:T(8,128)(2,1)S(1)} %get-tuple-element.23.near, ...), custom_call_target="tpu_custom_call" | custom-call | flops 3221225472 | bytes 4194304 | tf_op jit(solution)/shard_map/inner/pallas_call | solution.py:391
  23.2 4.3 %outer.1 = (bf16[256,1152]{1,0:T(8,128)(2,1)S(1)}, bf16[256,1152]{1,0:T(8,128)(2,1)S(1)}, bf16[4,272,256]{2,1,0:T(8,128)(2,1)}, bf16[4,8,16,256]{3,2,1,0:T(8,128)(2,1)}) custom-call(s32[1]{0:T(128)} %bitcast.refs_13_.core, bf16[4,8,16,256]{3,2,1,0:T(8,128)(2,1)S(1)} %copy-done, ...), custom_call_target="tpu_custom_call", output_to_operand_aliasing={{3}: (12, {})} | custom-call | flops 4294967296 | bytes 4194304 | tf_op jit(solution)/shard_map/outer/pallas_call | solution.py:391
  27.5 0.6 collective-permute-start.4
  28.0 1.6 %collective-permute-done.4.got = bf16[256,1152]{1,0:T(8,128)(2,1)S(1)} collective-permute-done((bf16[256,1152]{1,0:T(8,128)(2,1)S(1)}, bf16[256,1152]{1,0:T(8,128)(2,1)S(1)}, u32[]{:S(2)}, u32[]{:S(2)}) %collective-permute-start.4) | collective-permute-done | bytes 589856 | tf_op jit(solution)/shard_map/ppermute | solution.py:456
  29.7 0.1 fold.1
  29.8 0.4 collective-permute-start.5
  30.2 0.7 %collective-permute-start.6 = (bf16[64,1152]{1,0:T(8,128)(2,1)S(1)}, bf16[64,1152]{1,0:T(8,128)(2,1)S(1)}, u32[]{:S(2)}, u32[]{:S(2)}) collective-permute-start(bf16[64,1152]{1,0:T(8,128)(2,1)S(1)} %get-tuple-element.39), channel_id=1, source_target_pairs={{0,8},{1,9},{2,10},{3,11},{4,12},{5,13},{6,14},{7,15},{8,0},{9,1},... | collective-permute-start | bytes 442376 | tf_op jit(solution)/shard_map/ppermute | solution.py:464
  30.9 2.2 %collective-permute-start.7 = (bf16[64,1152]{1,0:T(8,128)(2,1)S(1)}, bf16[64,1152]{1,0:T(8,128)(2,1)S(1)}, u32[]{:S(2)}, u32[]{:S(2)}) collective-permute-start(bf16[64,1152]{1,0:T(8,128)(2,1)S(1)} %get-tuple-element.40), channel_id=1, source_target_pairs={{0,24},{1,25},{2,26},{3,27},{4,28},{5,29},{6,30},{7,31},{8,16},{9,... | collective-permute-start | bytes 442376 | tf_op jit(solution)/shard_map/ppermute | solution.py:464
  33.1 2.9 %tail.1 = (bf16[4,8,16,256]{3,2,1,0:T(8,128)(2,1)}, f32[64,1152]{1,0:T(8,128)S(1)}) custom-call(bf16[4,272,256]{2,1,0:T(8,128)(2,1)S(1)} %copy-done.4, bf16[4,8,16,256]{3,2,1,0:T(8,128)(2,1)S(1)} %copy-done.1, bf16[4,9,32,128]{3,2,1,0:T(8,128)(2,1)S(1)} %get-tuple-element.24.refs_12_.far, ...), custom_call_target="tpu_custom_call", output_to_operand_aliasing={{1}: (4, {})} | custom-call | flops 2147483648 | bytes 4194304 | tf_op jit(solution)/shard_map/tail/pallas_call | solution.py:391
  36.0 0.4 collective-permute-done.5.one
  36.4 1.2 %collective-permute-done.6.two = bf16[64,1152]{1,0:T(8,128)(2,1)S(1)} collective-permute-done((bf16[64,1152]{1,0:T(8,128)(2,1)S(1)}, bf16[64,1152]{1,0:T(8,128)(2,1)S(1)}, u32[]{:S(2)}, u32[]{:S(2)}) %collective-permute-start.6) | collective-permute-done | bytes 147488 | tf_op jit(solution)/shard_map/ppermute | solution.py:464
  37.7 2.7 %collective-permute-done.7.three = bf16[64,1152]{1,0:T(8,128)(2,1)S(1)} collective-permute-done((bf16[64,1152]{1,0:T(8,128)(2,1)S(1)}, bf16[64,1152]{1,0:T(8,128)(2,1)S(1)}, u32[]{:S(2)}, u32[]{:S(2)}) %collective-permute-start.7) | collective-permute-done | bytes 147488 | tf_op jit(solution)/shard_map/ppermute | solution.py:464
  40.4 11.3 %all_to_all.10.shares = bf16[8,8,1152]{2,1,0:T(8,128)(2,1)S(1)} all-to-all(bf16[8,8,1152]{2,1,0:T(8,128)(2,1)S(1)} %join.1), channel_id=1, replica_groups={{0,1,2,3,4,5,6,7},{8,9,10,11,12,13,14,15},{16,17,18,19,20,21,22,23},{24..., dimensions={0} | all-to-all | bytes 294912 | tf_op jit(solution)/shard_map/all_to_all | solution.py:470
  51.8 11.8 %all_to_all.11.shares = bf16[8,8,1152]{2,1,0:T(8,128)(2,1)S(1)} all-to-all(bf16[8,8,1152]{2,1,0:T(8,128)(2,1)S(1)} %share.1), channel_id=1, replica_groups=mesh['ens'=2,'lat'=4,'lon'=32] {'ens','lat'}, dimensions={0} | all-to-all | bytes 294912 | tf_op jit(solution)/shard_map/all_to_all | solution.py:474
  63.5 0.7 %place.1 = f32[9,8,256]{2,1,0:T(8,128)} custom-call(bf16[8,8,1152]{2,1,0:T(8,128)(2,1)S(1)} %all_to_all.11.shares), custom_call_target="tpu_custom_call" | custom-call | bytes 1048576 | tf_op jit(solution)/shard_map/place/pallas_call | solution.py:391
  (24 shorter events, 0.7 us)
Async XLA Ops:
  1.7 13.5 %collective-permute-start = (bf16[4,12,8,256]{3,2,1,0:T(8,128)(2,1)S(1)}, bf16[4,12,8,256]{3,2,1,0:T(8,128)(2,1)S(1)}, u32[]{:S(2)}, u32[]{:S(2)}) collective-permute-start(bf16[4,12,8,256]{3,2,1,0:T(8,128)(2,1)S(1)} %get-tuple-element.25), channel_id=1, source_target_pairs={{0,1},{1,2},{2,3},{3,4},{4,5},{5,6},{6,7},{7,8},{8,9},{9,10},{10,1... | collective-permute-start | bytes 589832 | tf_op jit(solution)/shard_map/ppermute | solution.py:424
  4.3 11.0 %collective-permute-start.1 = (bf16[4,12,8,256]{3,2,1,0:T(8,128)(2,1)S(1)}, bf16[4,12,8,256]{3,2,1,0:T(8,128)(2,1)S(1)}, u32[]{:S(2)}, u32[]{:S(2)}) collective-permute-start(bf16[4,12,8,256]{3,2,1,0:T(8,128)(2,1)S(1)} %get-tuple-element.26), channel_id=1, source_target_pairs={{1,0},{2,1},{3,2},{4,3},{5,4},{6,5},{7,6},{8,7},{9,8},{10,9},{11,1... | collective-permute-start | bytes 589832 | tf_op jit(solution)/shard_map/ppermute | solution.py:425
  10.7 2.5 %copy-start = (bf16[4,8,16,256]{3,2,1,0:T(8,128)(2,1)S(1)}, bf16[4,8,16,256]{3,2,1,0:T(8,128)(2,1)}, u32[]{:S(2)}) copy-start(bf16[4,8,16,256]{3,2,1,0:T(8,128)(2,1)} %x.9) | copy-start | bytes 786436
  10.8 2.5 %copy-start.2 = (s32[32,3]{0,1:T(4,128)S(1)}, s32[32,3]{0,1:T(4,128)}, u32[]{:S(2)}) copy-start(s32[32,3]{0,1:T(4,128)} %param.11) | copy-start | bytes 1156
  10.8 2.5 %copy-start.3 = (s32[32]{0:T(128)S(1)}, s32[32]{0:T(128)}, u32[]{:S(2)}) copy-start(s32[32]{0:T(128)} %cycles.1) | copy-start | bytes 388
  12.7 2.5 %copy-start.1 = (bf16[4,8,16,256]{3,2,1,0:T(8,128)(2,1)S(1)}, bf16[4,8,16,256]{3,2,1,0:T(8,128)(2,1)}, u32[]{:S(2)}) copy-start(bf16[4,8,16,256]{3,2,1,0:T(8,128)(2,1)} %out_grad.5) | copy-start | bytes 786436
  15.4 7.8 %collective-permute-start.3 = (bf16[4,11,8,256]{3,2,1,0:T(8,128)(2,1)S(1)}, bf16[4,11,8,256]{3,2,1,0:T(8,128)(2,1)S(1)}, u32[]{:S(2)}, u32[]{:S(2)}) collective-permute-start(bf16[4,11,8,256]{3,2,1,0:T(8,128)(2,1)S(1)} %get-tuple-element.28), channel_id=1, source_target_pairs={{32,64},{64,32},{33,65},{65,33},{34,66},{66,34},{35,67},{67,35},{3... | collective-permute-start | bytes 540680 | tf_op jit(solution)/shard_map/ppermute | solution.py:446
  19.6 3.5 %collective-permute-start.2 = (bf16[4,11,8,256]{3,2,1,0:T(8,128)(2,1)S(1)}, bf16[4,11,8,256]{3,2,1,0:T(8,128)(2,1)S(1)}, u32[]{:S(2)}, u32[]{:S(2)}) collective-permute-start(bf16[4,11,8,256]{3,2,1,0:T(8,128)(2,1)S(1)} %get-tuple-element.27.after), channel_id=1, source_target_pairs={{0,32},{32,0},{64,96},{96,64},{1,33},{33,1},{65,97},{97,65},{2,34}... | collective-permute-start | bytes 540680 | tf_op jit(solution)/shard_map/ppermute | solution.py:447
  27.4 5.7 %copy-start.4 = (bf16[4,272,256]{2,1,0:T(8,128)(2,1)S(1)}, bf16[4,272,256]{2,1,0:T(8,128)(2,1)}, u32[]{:S(2)}) copy-start(bf16[4,272,256]{2,1,0:T(8,128)(2,1)} %get-tuple-element.32.grads_in) | copy-start | bytes 1671172
  27.5 2.2 %collective-permute-start.4 = (bf16[256,1152]{1,0:T(8,128)(2,1)S(1)}, bf16[256,1152]{1,0:T(8,128)(2,1)S(1)}, u32[]{:S(2)}, u32[]{:S(2)}) collective-permute-start(bf16[256,1152]{1,0:T(8,128)(2,1)S(1)} %get-tuple-element.34), channel_id=1, source_target_pairs={{0,32},{32,0},{64,96},{96,64},{1,33},{33,1},{65,97},{97,65},{2,34}... | collective-permute-start | bytes 1769480 | tf_op jit(solution)/shard_map/ppermute | solution.py:456
  29.8 6.6 %collective-permute-start.5 = (bf16[64,1152]{1,0:T(8,128)(2,1)S(1)}, bf16[64,1152]{1,0:T(8,128)(2,1)S(1)}, u32[]{:S(2)}, u32[]{:S(2)}) collective-permute-start(bf16[64,1152]{1,0:T(8,128)(2,1)S(1)} %get-tuple-element.38), channel_id=1, source_target_pairs={{0,16},{1,17},{2,18},{3,19},{4,20},{5,21},{6,22},{7,23},{8,24},{9,... | collective-permute-start | bytes 442376 | tf_op jit(solution)/shard_map/ppermute | solution.py:464
  30.2 7.4 %collective-permute-start.6 = (bf16[64,1152]{1,0:T(8,128)(2,1)S(1)}, bf16[64,1152]{1,0:T(8,128)(2,1)S(1)}, u32[]{:S(2)}, u32[]{:S(2)}) collective-permute-start(bf16[64,1152]{1,0:T(8,128)(2,1)S(1)} %get-tuple-element.39), channel_id=1, source_target_pairs={{0,8},{1,9},{2,10},{3,11},{4,12},{5,13},{6,14},{7,15},{8,0},{9,1},... | collective-permute-start | bytes 442376 | tf_op jit(solution)/shard_map/ppermute | solution.py:464
  30.9 9.4 %collective-permute-start.7 = (bf16[64,1152]{1,0:T(8,128)(2,1)S(1)}, bf16[64,1152]{1,0:T(8,128)(2,1)S(1)}, u32[]{:S(2)}, u32[]{:S(2)}) collective-permute-start(bf16[64,1152]{1,0:T(8,128)(2,1)S(1)} %get-tuple-element.40), channel_id=1, source_target_pairs={{0,24},{1,25},{2,26},{3,27},{4,28},{5,29},{6,30},{7,31},{8,16},{9,... | collective-permute-start | bytes 442376 | tf_op jit(solution)/shard_map/ppermute | solution.py:464
